TPU v7x, 256 devices: a whole 4x4x8 slice. The times are simulated.
256 devices in a mesh: dp: 32 (over z, x), expert: 8 (over y, core).
Axes of the slice: x: 4, y: 4, z: 8, core: 2. Of those that a mesh axis runs over, the one named last changes fastest.
Arguments:
- grad_out: bfloat16 [32768, 1536], P(('dp', 'expert')), may hold values from -6 to 6
- expert_ids: int32 [32768, 2], P(('dp', 'expert')), may hold values from 0 to 7, all different within a row; in each aligned block of 128 rows (0 to 127, 128 to 255, ...) at most 48 rows name the same one
- gates: float32 [32768, 2], P(('dp', 'expert')), may hold values from 0.1 to 1
- routed_pre: bfloat16 [32, 8, 384, 3072], P('dp', 'expert'), may hold values from -6 to 6
- routed_down: bfloat16 [8, 3072, 1536], P('expert', 'dp'), may hold values from -0.109375 to 0.109375
- shared_pre: bfloat16 [32768, 6144], P('dp', 'expert'), may hold values from -6 to 6
- shared_down: bfloat16 [6144, 1536], P(('expert', 'dp')), may hold values from -0.078125 to 0.078125
Outputs:
- routed_pre_grad: bfloat16 [32, 8, 384, 3072], P('dp', 'expert')
- routed_down_grad: float32 [8, 3072, 1536], P('expert', 'dp')
- shared_pre_grad: bfloat16 [32768, 6144], P('dp', 'expert')
- shared_down_grad: float32 [6144, 1536], P(('expert', 'dp'))
- gate_grad: float32 [32768, 2], P(('dp', 'expert'))
Inputs may be any that keep to these rules, and one draw needn't show every extreme that they name: `expert_ids`: each row names two different experts. Among the 128 rows of one device no expert is named more than 48 times, and in every draw some expert is named exactly 48 times by the rows of some device.
All inputs are finite; a program needn't handle non-finite values.
Results may differ from a plain program's by a relative error of at most 0.015.
Values may be sent and summed in bfloat16 or wider, within the bound.
No kernel may reach another device: no remote copies, remote signals or barrier semaphores. Data moves between devices by JAX's collectives and lax.ppermute only.
A program may use at most 128 MiB of HBM per device.

v0:
```python
import jax
import jax.numpy as jnp
from jax import lax
from jax.experimental import pallas as pl
from jax.experimental.pallas import tpu as pltpu
from jax.sharding import Mesh
from jax.sharding import PartitionSpec as P


DP = ("z", "x")
EXPERT = ("y", "c")
DP_EXPERT = ("z", "x", "y", "c")
EXPERT_DP = ("y", "c", "z", "x")
NZ, NX, NY, NC = 8, 4, 4, 2


SQRT_TWO_PI = 0.7978845608028654
BF = jnp.bfloat16
F32 = jnp.float32


def hop(a, axis, by):
    n = lax.axis_size(axis)
    return lax.ppermute(a, axis, [(i, (i + by) % n) for i in range(n)])


def gelu_pair(inputs):
    cubic = inputs * inputs * inputs
    tangent = jnp.tanh(SQRT_TWO_PI * (inputs + 0.044715 * cubic))
    value = 0.5 * inputs * (1.0 + tangent)
    slope = 0.5 * (1.0 + tangent) + 0.5 * inputs * (1.0 - tangent * tangent) * SQRT_TWO_PI * (
        1.0 + 3.0 * 0.044715 * inputs * inputs
    )
    return (value, slope)


def added(a, b):
    return (a.astype(F32) + b.astype(F32)).astype(BF)


def gather_eight(a, axis, cut):
    right = [a]
    left = [a]
    for _ in range(1, 4):
        right.append(hop(right[-1], axis, 1))
        left.append(hop(left[-1], axis, -1))
    far = (hop(cut(right[3])[0], axis, 1), hop(cut(left[3])[1], axis, -1))
    return right[0], right[1], right[2], right[3], far, left[3], left[2], left[1]


def cut_rows(a):
    half = a.shape[0] // 2
    return a[:half], a[half:]


def sum_ring(block, n, axis, cut, join):
    far_first, far_second = cut(block(n // 2))
    right = hop(far_first, axis, 1)
    left = hop(far_second, axis, -1)
    for r in range(n // 2 - 1, 0, -1):
        mine_r, mine_l = block(r), block(n - r)
        if r == n // 2 - 1:
            a, b = cut(mine_r)
            send_r = join(added(a, right), b)
            a, b = cut(mine_l)
            send_l = join(a, added(b, left))
        else:
            send_r = added(mine_r, right)
            send_l = added(mine_l, left)
        right = hop(send_r, axis, 1)
        left = hop(send_l, axis, -1)
    return block(0).astype(F32) + right.astype(F32) + left.astype(F32)


def join_rows(a, b):
    return jnp.concatenate([a, b], axis=0)


def dispatch_kernel(sc, mine, partner, grp, recv, scal, gate):
    owner, core = sc[0], sc[1]
    tok, cap = grp.shape[0] // 2, recv.shape[0] // 2
    me = owner.astype(F32)
    earlier = lax.broadcasted_iota(jnp.int32, (tok, tok), 0)
    later = lax.broadcasted_iota(jnp.int32, (tok, tok), 1)
    tri = jnp.where(earlier < later, 1.0, 0.0).astype(BF)
    place = lax.broadcasted_iota(jnp.int32, (cap, tok), 0)
    for ref, at in ((mine, core), (partner, 1 - core)):
        tokens = ref[0, :tok, :]
        meta = ref[0, tok:, :tok].astype(F32)
        g0, g1, i0, i1 = (meta[k : k + 1, :] for k in range(4))
        hit0, hit1 = (i0 == me), (i1 == me)
        named = jnp.where(hit0, 1.0, jnp.where(hit1, 1.0, 0.0))
        picked = jnp.where(hit0, g0, jnp.where(hit1, g1, 0.0))
        rank = lax.dot_general(
            jnp.broadcast_to(named, (8, tok)).astype(BF),
            tri,
            (((1,), (0,)), ((), ())),
            preferred_element_type=F32,
        )[0:1]
        rank = jnp.where(named > 0.0, rank, -1.0).astype(jnp.int32)
        onehot = jnp.where(place == rank, 1.0, 0.0)
        rows = lax.dot_general(
            onehot.astype(BF), tokens, (((1,), (0,)), ((), ())), preferred_element_type=F32
        )
        weight = jnp.sum(onehot * picked, axis=1, keepdims=True)
        grp[pl.ds(pl.multiple_of(at * tok, tok), tok), :] = tokens
        slot = pl.ds(pl.multiple_of(at * cap, cap), cap)
        recv[slot, :] = rows.astype(BF)
        scal[slot, :] = (weight * rows).astype(BF)
        gate[slot, :] = weight


def dispatch(scalars, mine, partner, tok, slots):
    width = mine.shape[2]
    cap2 = slots // NY
    taken = pl.BlockSpec((1, *mine.shape[1:]), lambda k: (k, 0, 0))

    def given(rows, cols):
        return pl.BlockSpec((rows, cols), lambda k: (k, 0))

    return pl.pallas_call(
        dispatch_kernel,
        name="dispatch",
        grid=(NY,),
        out_shape=(
            jax.ShapeDtypeStruct((NY * NC * tok, width), BF),
            jax.ShapeDtypeStruct((slots, width), BF),
            jax.ShapeDtypeStruct((slots, width), BF),
            jax.ShapeDtypeStruct((slots, 1), F32),
        ),
        in_specs=[pl.BlockSpec(memory_space=pltpu.SMEM), taken, taken],
        out_specs=(given(NC * tok, width), given(cap2, width), given(cap2, width), given(cap2, 1)),
        compiler_params=pltpu.CompilerParams(vmem_limit_bytes=24 << 20),
        cost_estimate=pl.CostEstimate(flops=200_000_000, bytes_accessed=10_000_000, transcendentals=0),
    )(scalars, mine, partner)


def terms_kernel(hidden, scal, tsh, ta, tb):
    out = lax.dot_general(
        hidden[...], scal[...], (((0,), (0,)), ((), ())), preferred_element_type=F32
    )
    nx, rows, half = tb.shape[1], hidden.shape[1] // tb.shape[1], tb.shape[3]
    out = out.astype(BF).reshape(nx, rows, 2 * half)
    ta[:, 0, :rows, :] = out[:, :, :half]
    tb[0, :, :rows, :] = out[:, :, half:]
    ta[:, 0, rows:, :] = tsh[0, :, :, :half]
    tb[0, :, rows:, :] = tsh[0, :, :, half:]


def terms(hidden, scal, tsh):
    slots, hid = hidden.shape
    width = scal.shape[1]
    rows, extra = hid // (NZ * NX), tsh.shape[2]
    tail = (rows + extra, width // 2)
    return pl.pallas_call(
        terms_kernel,
        name="terms",
        grid=(NZ,),
        out_shape=(
            jax.ShapeDtypeStruct((NX, NZ, *tail), BF),
            jax.ShapeDtypeStruct((NZ, NX, *tail), BF),
        ),
        in_specs=[
            pl.BlockSpec((slots, hid // NZ), lambda k: (0, k)),
            pl.BlockSpec((slots, width), lambda k: (0, 0)),
            pl.BlockSpec((1, NX, extra, width), lambda k: (k, 0, 0, 0)),
        ],
        out_specs=(
            pl.BlockSpec((NX, 1, *tail), lambda k: (0, k, 0, 0)),
            pl.BlockSpec((1, NX, *tail), lambda k: (k, 0, 0, 0)),
        ),
        compiler_params=pltpu.CompilerParams(vmem_limit_bytes=24 << 20),
        cost_estimate=pl.CostEstimate(
            flops=2 * slots * hid * width, bytes_accessed=18_000_000, transcendentals=0
        ),
    )(hidden, scal, tsh)


RAW_STEPS = 3
ARRIVAL = (0, 1, 7, 2, 6, 3, 5, 4)


def raw_kernel(sc, rows, gate, pre, a_ref, *refs):
    *b_refs, _, _, out, wsh, score, whole, small = refs
    n_rows = whole.shape[0] // NX
    extra = small.shape[0] // NX
    half = whole.shape[1] // 2

    @pl.when(pl.program_id(0) == 0)
    def _():
        for k in range(NX):
            b_ref, i = (b_refs[0], k) if len(b_refs) == 1 else (b_refs[k // 2], k % 2)
            whole[k * n_rows : (k + 1) * n_rows, :half] = a_ref[k, 0, :n_rows, :]
            whole[k * n_rows : (k + 1) * n_rows, half:] = b_ref[i, :n_rows, :]
            small[k * extra : (k + 1) * extra, :half] = a_ref[k, 0, n_rows:, :].astype(F32)
            small[k * extra : (k + 1) * extra, half:] = b_ref[i, n_rows:, :].astype(F32)
        wsh[...] = small[...].astype(BF)

    raw = lax.dot_general(
        rows[...], whole[...], (((1,), (1,)), ((), ())), preferred_element_type=F32
    )
    value, slope = gelu_pair(pre[...].astype(F32))
    out[...] = (gate[...] * raw * slope).astype(BF)
    score[...] = jnp.sum(value * raw, axis=1, keepdims=True)


def raw_block(scalars, rows, gate, pre, a_whole, b_piece, carried):
    slots, width = rows.shape
    hid = pre.shape[1]
    block, step = hid // NZ, slots // RAW_STEPS
    n_rows = block // NX
    extra = a_whole.shape[2] - n_rows
    half = width // 2
    b_list = list(b_piece) if isinstance(b_piece, tuple) else [b_piece]
    in_specs = [
        pl.BlockSpec((step, width), lambda i, sc: (i, 0)),
        pl.BlockSpec((step, 1), lambda i, sc: (i, 0)),
        pl.BlockSpec((step, block), lambda i, sc: (i, sc[0])),
        pl.BlockSpec((NX, 1, n_rows + extra, half), lambda i, sc: (0, sc[0], 0, 0)),
    ]
    in_specs += [pl.BlockSpec(b.shape, lambda i, sc: (0, 0, 0)) for b in b_list]
    args = [rows, gate, pre, a_whole, *b_list]
    aliases = {}
    in_specs += [pl.BlockSpec(memory_space=pl.ANY)] * 2
    if carried is not None:
        aliases = {1 + len(args): 0, 2 + len(args): 1}
        args += list(carried)
    else:
        args += [gate, gate]
    return pl.pallas_call(
        raw_kernel,
        name="raw",
        out_shape=(
            jax.ShapeDtypeStruct((slots, hid), BF),
            jax.ShapeDtypeStruct((NZ * NX * extra, width), BF),
            jax.ShapeDtypeStruct((slots, 1), F32),
        ),
        grid_spec=pltpu.PrefetchScalarGridSpec(
            num_scalar_prefetch=1,
            grid=(RAW_STEPS,),
            in_specs=in_specs,
            out_specs=(
                pl.BlockSpec((step, block), lambda i, sc: (i, sc[0])),
                pl.BlockSpec((NX * extra, width), lambda i, sc: (sc[0], 0)),
                pl.BlockSpec((step, 1), lambda i, sc: (i, 0)),
            ),
            scratch_shapes=[pltpu.VMEM((block, width), BF), pltpu.VMEM((NX * extra, width), F32)],
        ),
        input_output_aliases=aliases,
        compiler_params=pltpu.CompilerParams(vmem_limit_bytes=16 << 20),
        cost_estimate=pl.CostEstimate(
            flops=2 * slots * block * width, bytes_accessed=5_000_000, transcendentals=slots * block
        ),
    )(scalars, *args)


def to_all(a, axis, n):
    many = jnp.broadcast_to(a[None], (n, *a.shape))
    return lax.all_to_all(many, axis, 0, 0, tiled=True)


def body(grad_out, expert_ids, gates, routed_pre, routed_down, shared_pre, shared_down):
    z, _, y, c = (lax.axis_index(a) for a in ("z", "x", "y", "c"))
    owner = y * NC + c
    n_exp = NY * NC
    tok, width = grad_out.shape
    slots = routed_pre.shape[2]
    cap = slots // n_exp
    half = width // 2

    shard = jnp.concatenate([routed_down[0], shared_down], axis=0)
    a_whole = lax.all_gather(shard[:, :half], "z")
    a_whole = lax.all_gather(a_whole, "x")
    b_pieces = gather_eight(to_all(shard[:, half:], "x", NX), "z", cut_rows)

    metas = jnp.concatenate([gates.astype(BF).T, expert_ids.astype(BF).T], axis=0)
    metas = jnp.pad(metas, ((0, 8 - metas.shape[0]), (0, width - tok)))
    mine = to_all(jnp.concatenate([grad_out, metas], axis=0), "y", NY)
    partner = hop(mine, "c", 1)

    pre = routed_pre[0, 0]
    hidden_b = gelu_pair(pre.astype(F32))[0].astype(BF)
    shared_b = gelu_pair(shared_pre.astype(F32))[0].astype(BF)

    scalars = jnp.stack([owner, c]).astype(jnp.int32)
    group_rows, recv_rows, scaled, gate_col = dispatch(scalars, mine, partner, tok, slots)

    shared_term = lax.dot_general(
        shared_b, group_rows, (((0,), (0,)), ((), ())), preferred_element_type=F32
    ).astype(BF)
    ta, tb = terms(hidden_b, scaled, shared_term.reshape(NZ, NX, -1, width))
    sum_a = lax.psum_scatter(ta.reshape(-1, half), "x", scatter_dimension=0, tiled=True)
    sum_a = lax.psum_scatter(sum_a, "z", scatter_dimension=0, tiled=True)
    sum_a = sum_a.astype(F32)

    def along(r):
        return lax.dynamic_index_in_dim(tb, (z + r) % NZ, 0, keepdims=False)

    sum_b = sum_ring(along, NZ, "z", cut_rows, join_rows).astype(BF)
    sum_b = lax.all_to_all(sum_b, "x", 0, 0, tiled=True).astype(F32).sum(axis=0)
    total = jnp.concatenate([sum_a, sum_b], axis=1)
    rows = routed_down.shape[1]

    carried, scores = None, []
    for j in ARRIVAL:
        sc = jnp.stack([(z + (NZ - j)) % NZ]).astype(jnp.int32)
        out, wsh, score = raw_block(sc, recv_rows, gate_col, pre, a_whole, b_pieces[j], carried)
        carried = (out, wsh)
        scores.append(score)
    routed_pre_grad, whole_shared = carried
    slot_score = sum(scores[1:], scores[0])
    returned = lax.all_to_all(slot_score.reshape(n_exp, cap), EXPERT, 0, 0, tiled=True)

    labels = jnp.arange(n_exp, dtype=jnp.int32)
    onehot = expert_ids[:, :, None] == labels[None, None, :]
    named = jnp.any(onehot, axis=1).astype(F32)
    order = jnp.arange(tok, dtype=jnp.int32)
    tri = (order[None, :] < order[:, None]).astype(F32)
    counts = lax.dot_general(tri, named, (((1,), (0,)), ((), ())), preferred_element_type=F32)
    rank = jnp.sum(jnp.where(onehot, counts[:, None, :], 0.0), axis=2).astype(jnp.int32)
    slot = expert_ids * cap + rank
    each = jnp.arange(slots, dtype=jnp.int32)
    gate_grad = jnp.sum(
        jnp.where(slot[:, :, None] == each[None, None, :], returned.reshape(1, 1, slots), 0.0), axis=2
    )

    raw_shared = lax.dot_general(
        group_rows, whole_shared, (((1,), (1,)), ((), ())), preferred_element_type=F32
    )
    shared_pre_grad = (raw_shared * gelu_pair(shared_pre.astype(F32))[1]).astype(BF)
    return (
        routed_pre_grad.reshape(routed_pre.shape),
        total[:rows].reshape(1, rows, width),
        shared_pre_grad,
        total[rows:],
        gate_grad,
    )


def solution(mesh):
    split = Mesh(mesh.devices.reshape(NZ, NX, NY, NC), ("z", "x", "y", "c"))
    placed = (
        P(DP_EXPERT, None),
        P(DP_EXPERT, None),
        P(DP_EXPERT, None),
        P(DP, EXPERT, None, None),
        P(EXPERT, DP, None),
        P(DP, EXPERT),
        P(EXPERT_DP, None),
    )
    return jax.shard_map(
        body,
        mesh=split,
        in_specs=placed,
        out_specs=(
            P(DP, EXPERT, None, None),
            P(EXPERT, DP, None),
            P(DP, EXPERT),
            P(EXPERT_DP, None),
            P(DP_EXPERT, None),
        ),
        check_vma=False,
    )
```

profile of v0, /device:TPU:8, one launch (start us, length us, event | category | flops | bytes accessed | tf_op | source)
XLA Modules:
  0.0 293.7 jit_solution(18238347958737311771)
XLA Ops:
  12.2 25.3 %all_to_all.24.mine = bf16[4,136,1536]{2,1,0:T(8,128)(2,1)} all-to-all(bf16[4,136,1536]{2,1,0:T(8,128)(2,1)S(1)} %broadcast_in_dim.26), channel_id=1, replica_groups=mesh['z'=8,'x'=4,'y'=4,'c'=2] {'y'}, dimensions={0} | all-to-all | bytes 3342336 | tf_op jit(solution)/shard_map/all_to_all | solution.py:259
  41.4 3.9 %dispatch.1 = (bf16[1024,1536]{1,0:T(8,128)(2,1)S(1)}, bf16[384,1536]{1,0:T(8,128)(2,1)S(1)}, bf16[384,1536]{1,0:T(8,128)(2,1)S(1)}, f32[384,1]{1,0:T(8,128)S(1)}) custom-call(s32[2]{0:T(128)S(1)} %pad_add_fusion.sc, bf16[4,136,1536]{2,1,0:T(8,128)(2,1)} %all_to_all.24.mine, bf16[4,136,1536]{2,1,0:T(8,128)(2,1)} %collective-permute-done.partner), custom_call_target="tpu_custom_call" | custom-call | flops 200000000 | bytes 10000000 | tf_op jit(solution)/shard_map/dispatch/pallas_call | solution.py:121
  45.3 3.0 %convolution_convert_fusion = bf16[768,1536]{1,0:T(8,128)(2,1)S(1)} fusion(bf16[1024,1536]{1,0:T(8,128)(2,1)S(1)} %get-tuple-element.53, bf16[1024,768]{1,0:T(8,128)(2,1)S(1)} %copy-done.13), kind=kOutput, calls=%fused_computation.18 | convolution fusion | flops 2424963072 | bytes 7077888 | tf_op jit(solution)/shard_map/dot_general | solution.py:288
  48.4 7.0 %terms.1 = (bf16[4,8,120,768]{3,2,1,0:T(8,128)(2,1)S(1)}, bf16[8,4,120,768]{3,2,1,0:T(8,128)(2,1)S(1)}) custom-call(bf16[384,3072]{1,0:T(8,128)(2,1)S(1)} %fusion.1.hidden, bf16[384,1536]{1,0:T(8,128)(2,1)S(1)} %get-tuple-element.52.scal, bf16[8,4,24,1536]{3,2,1,0:T(8,128)(2,1)S(1)} %bitcast.79), custom_call_target="tpu_custom_call" | custom-call | flops 3623878656 | bytes 18000000 | tf_op jit(solution)/shard_map/terms/pallas_call | solution.py:155
  60.4 19.4 %all-gather.5.cloned.1.call-done = bf16[960,768]{1,0:T(8,128)(2,1)} async-done(((bf16[120,768]{1,0:T(8,128)(2,1)}), bf16[960,768]{1,0:T(8,128)(2,1)}) %all-gather.5.cloned.1.call-update) | async-done | bytes 1474576 | tf_op jit(solution)/shard_map/all_gather | solution.py:272
  84.1 5.5 %collective-permute-done.13 = bf16[2,120,768]{2,1,0:T(8,128)(2,1)S(1)} collective-permute-done((bf16[2,120,768]{2,1,0:T(8,128)(2,1)S(1)}, bf16[2,120,768]{2,1,0:T(8,128)(2,1)S(1)}, u32[]{:S(2)}, u32[]{:S(2)}) %collective-permute-start.13) | collective-permute-done | bytes 368672 | tf_op jit(solution)/shard_map/ppermute | solution.py:24
  89.6 2.9 collective-permute-done.9
  97.5 3.2 %collective-permute-start.14 = (bf16[4,120,768]{2,1,0:T(8,128)(2,1)}, bf16[4,120,768]{2,1,0:T(8,128)(2,1)}, u32[]{:S(2)}, u32[]{:S(2)}) collective-permute-start(bf16[4,120,768]{2,1,0:T(8,128)(2,1)} %pad_maximum_fusion.1), channel_id=1, source_target_pairs={{0,224},{32,0},{64,32},{96,64},{128,96},{160,128},{192,160},{224,1... | collective-permute-start | bytes 2211848 | tf_op jit(solution)/shard_map/ppermute | solution.py:24
  100.7 9.3 %collective-permute-done.10 = bf16[4,120,768]{2,1,0:T(8,128)(2,1)} collective-permute-done((bf16[4,120,768]{2,1,0:T(8,128)(2,1)}, bf16[4,120,768]{2,1,0:T(8,128)(2,1)}, u32[]{:S(2)}, u32[]{:S(2)}) %collective-permute-start.10) | collective-permute-done | bytes 737312 | tf_op jit(solution)/shard_map/ppermute | solution.py:24
  113.4 4.2 %all-to-all-start.1 = ((bf16[4,120,768]{2,1,0:T(8,128)(2,1)}), bf16[4,120,768]{2,1,0:T(8,128)(2,1)}, u32[]{:S(2)}, u32[]{:S(2)}) async-start(bf16[4,120,768]{2,1,0:T(8,128)(2,1)} %broadcast_in_dim.46), calls=%async_computation.1 | async-start | bytes 1474560 | tf_op jit(solution)/shard_map/all_to_all | solution.py:259
  117.6 14.7 %all-to-all-done.1.refs_0_ = bf16[4,120,768]{2,1,0:T(8,128)(2,1)} async-done(((bf16[4,120,768]{2,1,0:T(8,128)(2,1)}), bf16[4,120,768]{2,1,0:T(8,128)(2,1)}, u32[]{:S(2)}, u32[]{:S(2)}) %all-to-all-start.1) | async-done | bytes 737312 | tf_op jit(solution)/shard_map/all_to_all | solution.py:259
  135.6 3.2 %fusion.26 = (bf16[4,120,768]{2,1,0:T(8,128)(2,1)}, bf16[4,120,768]{2,1,0:T(8,128)(2,1)}) fusion(bf16[4,120,768]{2,1,0:T(8,128)(2,1)} %collective-permute-done.11, bf16[8,4,120,768]{3,2,1,0:T(8,128)(2,1)} %copy-done.6, s32[]{:T(128)S(6)} %select_n.96, bf16[4,120,768]{2,1,0:T(8,128)(2,1)} %collective-permute-done.14, s32[]{:T(128)S(6)} %select_n.101), kind=kLoop, calls=%fused_computation.40 | loop fusion | flops 2949120 | bytes 4423688 | tf_op jit(solution)/shard_map/convert_element_type | solution.py:38
  140.9 8.2 %collective-permute-done.1.refs_0_ = bf16[4,120,768]{2,1,0:T(8,128)(2,1)} collective-permute-done((bf16[4,120,768]{2,1,0:T(8,128)(2,1)}, bf16[4,120,768]{2,1,0:T(8,128)(2,1)}, u32[]{:S(2)}, u32[]{:S(2)}) %collective-permute-start.1) | collective-permute-done | bytes 737312 | tf_op jit(solution)/shard_map/ppermute | solution.py:24
  149.1 4.4 %collective-permute-done.5.refs_0_ = bf16[4,120,768]{2,1,0:T(8,128)(2,1)} collective-permute-done((bf16[4,120,768]{2,1,0:T(8,128)(2,1)}, bf16[4,120,768]{2,1,0:T(8,128)(2,1)}, u32[]{:S(2)}, u32[]{:S(2)}) %collective-permute-start.5) | collective-permute-done | bytes 737312 | tf_op jit(solution)/shard_map/ppermute | solution.py:24
  153.5 3.0 %collective-permute-start.6 = (bf16[4,120,768]{2,1,0:T(8,128)(2,1)}, bf16[4,120,768]{2,1,0:T(8,128)(2,1)}, u32[]{:S(2)}, u32[]{:S(2)}) collective-permute-start(bf16[4,120,768]{2,1,0:T(8,128)(2,1)} %collective-permute-done.5.refs_0_), channel_id=1, source_target_pairs={{0,224},{32,0},{64,32},{96,64},{128,96},{160,128},{192,160},{224,1... | collective-permute-start | bytes 2211848 | tf_op jit(solution)/shard_map/ppermute | solution.py:24
  156.5 12.8 %collective-permute-done.15 = bf16[4,120,768]{2,1,0:T(8,128)(2,1)} collective-permute-done((bf16[4,120,768]{2,1,0:T(8,128)(2,1)}, bf16[4,120,768]{2,1,0:T(8,128)(2,1)}, u32[]{:S(2)}, u32[]{:S(2)}) %collective-permute-start.15) | collective-permute-done | bytes 737312 | tf_op jit(solution)/shard_map/ppermute | solution.py:24
  171.7 3.0 %collective-permute-start.16 = (bf16[4,120,768]{2,1,0:T(8,128)(2,1)}, bf16[4,120,768]{2,1,0:T(8,128)(2,1)}, u32[]{:S(2)}, u32[]{:S(2)}) collective-permute-start(bf16[4,120,768]{2,1,0:T(8,128)(2,1)} %fusion.24), channel_id=1, source_target_pairs={{0,224},{32,0},{64,32},{96,64},{128,96},{160,128},{192,160},{224,1... | collective-permute-start | bytes 2211848 | tf_op jit(solution)/shard_map/ppermute | solution.py:24
  174.8 10.3 %collective-permute-done.6.refs_0_ = bf16[4,120,768]{2,1,0:T(8,128)(2,1)} collective-permute-done((bf16[4,120,768]{2,1,0:T(8,128)(2,1)}, bf16[4,120,768]{2,1,0:T(8,128)(2,1)}, u32[]{:S(2)}, u32[]{:S(2)}) %collective-permute-start.6) | collective-permute-done | bytes 737312 | tf_op jit(solution)/shard_map/ppermute | solution.py:24
  185.1 3.0 %collective-permute-start.7 = (bf16[4,120,768]{2,1,0:T(8,128)(2,1)}, bf16[4,120,768]{2,1,0:T(8,128)(2,1)}, u32[]{:S(2)}, u32[]{:S(2)}) collective-permute-start(bf16[4,120,768]{2,1,0:T(8,128)(2,1)} %collective-permute-done.6.refs_0_), channel_id=1, source_target_pairs={{0,224},{32,0},{64,32},{96,64},{128,96},{160,128},{192,160},{224,1... | collective-permute-start | bytes 2211848 | tf_op jit(solution)/shard_map/ppermute | solution.py:24
  188.1 25.1 %collective-permute-done.16 = bf16[4,120,768]{2,1,0:T(8,128)(2,1)} collective-permute-done((bf16[4,120,768]{2,1,0:T(8,128)(2,1)}, bf16[4,120,768]{2,1,0:T(8,128)(2,1)}, u32[]{:S(2)}, u32[]{:S(2)}) %collective-permute-start.16) | collective-permute-done | bytes 737312 | tf_op jit(solution)/shard_map/ppermute | solution.py:24
  215.9 4.2 %all-to-all-start.2 = ((bf16[4,120,768]{2,1,0:T(8,128)(2,1)}), bf16[4,120,768]{2,1,0:T(8,128)(2,1)}, u32[]{:S(2)}, u32[]{:S(2)}) async-start(bf16[4,120,768]{2,1,0:T(8,128)(2,1)} %fusion.28), calls=%async_computation.4 | async-start | bytes 1474560 | tf_op jit(solution)/shard_map/all_to_all | solution.py:300
  227.4 3.7 %collective-permute-start.8 = (bf16[2,120,768]{2,1,0:T(8,128)(2,1)}, bf16[2,120,768]{2,1,0:T(8,128)(2,1)}, u32[]{:S(2)}, u32[]{:S(2)}) collective-permute-start(bf16[2,120,768]{2,1,0:T(8,128)(2,1)} %slice.69), channel_id=1, source_target_pairs={{0,224},{32,0},{64,32},{96,64},{128,96},{160,128},{192,160},{224,1... | collective-permute-start | bytes 1105928 | tf_op jit(solution)/shard_map/ppermute | solution.py:24
  236.7 3.9 %raw.8 = (bf16[384,3072]{1,0:T(8,128)(2,1)}, bf16[768,1536]{1,0:T(8,128)(2,1)S(1)}, f32[384,1]{1,0:T(8,128)S(1)}) custom-call(s32[1]{0:T(128)} %bitcast.15.sc, bf16[384,1536]{1,0:T(8,128)(2,1)S(1)} %get-tuple-element.35.rows, f32[384,1]{1,0:T(8,128)S(1)} %copy-done.5, bf16[384,3072]{1,0:T(8,128)(2,1)S(1)} %bitcast.70, bf16[4,8,120,768]{3,2,1,0:T(8,128)(2,1)S(1)} %bitcast.62, ...), custom_call_target="tpu_custom_call" | custom-call | flops 452984832 | bytes 5000000 | tf_op jit(solution)/shard_map/raw/pallas_call | solution.py:230
  240.6 3.7 %raw.9 = (bf16[384,3072]{1,0:T(8,128)(2,1)}, bf16[768,1536]{1,0:T(8,128)(2,1)S(1)}, f32[384,1]{1,0:T(8,128)S(1)}) custom-call(s32[1]{0:T(128)} %bitcast.14.sc, bf16[384,1536]{1,0:T(8,128)(2,1)S(1)} %get-tuple-element.35.rows, f32[384,1]{1,0:T(8,128)S(1)} %copy-done.5, bf16[384,3072]{1,0:T(8,128)(2,1)S(1)} %bitcast.71, ...), custom_call_target="tpu_custom_call", output_to_operand_aliasing={{0}: (6, {}), {1}: (7, {})} | custom-call | flops 452984832 | bytes 5000000 | tf_op jit(solution)/shard_map/raw/pallas_call | solution.py:230
  244.3 3.7 %raw.10 = (bf16[384,3072]{1,0:T(8,128)(2,1)}, bf16[768,1536]{1,0:T(8,128)(2,1)S(1)}, f32[384,1]{1,0:T(8,128)S(1)}) custom-call(s32[1]{0:T(128)} %bitcast.13.sc, bf16[384,1536]{1,0:T(8,128)(2,1)S(1)} %get-tuple-element.35.rows, f32[384,1]{1,0:T(8,128)S(1)} %copy-done.5, bf16[384,3072]{1,0:T(8,128)(2,1)S(1)} %bitcast.72, ...), custom_call_target="tpu_custom_call", output_to_operand_aliasing={{0}: (6, {}), {1}: (7, {})} | custom-call | flops 452984832 | bytes 5000000 | tf_op jit(solution)/shard_map/raw/pallas_call | solution.py:230
  248.0 3.7 %raw.11 = (bf16[384,3072]{1,0:T(8,128)(2,1)}, bf16[768,1536]{1,0:T(8,128)(2,1)S(1)}, f32[384,1]{1,0:T(8,128)S(1)}) custom-call(s32[1]{0:T(128)} %bitcast.12.sc, bf16[384,1536]{1,0:T(8,128)(2,1)S(1)} %get-tuple-element.35.rows, f32[384,1]{1,0:T(8,128)S(1)} %copy-done.5, bf16[384,3072]{1,0:T(8,128)(2,1)S(1)} %bitcast.73, ...), custom_call_target="tpu_custom_call", output_to_operand_aliasing={{0}: (6, {}), {1}: (7, {})} | custom-call | flops 452984832 | bytes 5000000 | tf_op jit(solution)/shard_map/raw/pallas_call | solution.py:230
  251.7 3.7 %raw.12 = (bf16[384,3072]{1,0:T(8,128)(2,1)}, bf16[768,1536]{1,0:T(8,128)(2,1)S(1)}, f32[384,1]{1,0:T(8,128)S(1)}) custom-call(s32[1]{0:T(128)} %bitcast.11.sc, bf16[384,1536]{1,0:T(8,128)(2,1)S(1)} %get-tuple-element.35.rows, f32[384,1]{1,0:T(8,128)S(1)} %copy-done.5, bf16[384,3072]{1,0:T(8,128)(2,1)S(1)} %bitcast.74, ...), custom_call_target="tpu_custom_call", output_to_operand_aliasing={{0}: (6, {}), {1}: (7, {})} | custom-call | flops 452984832 | bytes 5000000 | tf_op jit(solution)/shard_map/raw/pallas_call | solution.py:230
  255.4 3.7 %raw.13 = (bf16[384,3072]{1,0:T(8,128)(2,1)}, bf16[768,1536]{1,0:T(8,128)(2,1)S(1)}, f32[384,1]{1,0:T(8,128)S(1)}) custom-call(s32[1]{0:T(128)} %bitcast.10.sc, bf16[384,1536]{1,0:T(8,128)(2,1)S(1)} %get-tuple-element.35.rows, f32[384,1]{1,0:T(8,128)S(1)} %copy-done.5, bf16[384,3072]{1,0:T(8,128)(2,1)S(1)} %bitcast.75, ...), custom_call_target="tpu_custom_call", output_to_operand_aliasing={{0}: (6, {}), {1}: (7, {})} | custom-call | flops 452984832 | bytes 5000000 | tf_op jit(solution)/shard_map/raw/pallas_call | solution.py:230
  259.1 3.7 %raw.14 = (bf16[384,3072]{1,0:T(8,128)(2,1)}, bf16[768,1536]{1,0:T(8,128)(2,1)S(1)}, f32[384,1]{1,0:T(8,128)S(1)}) custom-call(s32[1]{0:T(128)} %bitcast.9.sc, bf16[384,1536]{1,0:T(8,128)(2,1)S(1)} %get-tuple-element.35.rows, f32[384,1]{1,0:T(8,128)S(1)} %copy-done.5, bf16[384,3072]{1,0:T(8,128)(2,1)S(1)} %bitcast.76, ...), custom_call_target="tpu_custom_call", output_to_operand_aliasing={{0}: (6, {}), {1}: (7, {})} | custom-call | flops 452984832 | bytes 5000000 | tf_op jit(solution)/shard_map/raw/pallas_call | solution.py:230
  262.8 3.7 %raw.15 = (bf16[384,3072]{1,0:T(8,128)(2,1)}, bf16[768,1536]{1,0:T(8,128)(2,1)S(1)}, f32[384,1]{1,0:T(8,128)S(1)}) custom-call(s32[1]{0:T(128)} %bitcast.sc, bf16[384,1536]{1,0:T(8,128)(2,1)S(1)} %get-tuple-element.35.rows, f32[384,1]{1,0:T(8,128)S(1)} %copy-done.5, bf16[384,3072]{1,0:T(8,128)(2,1)S(1)} %bitcast.77, ...), custom_call_target="tpu_custom_call", output_to_operand_aliasing={{0}: (7, {}), {1}: (8, {})} | custom-call | flops 452984832 | bytes 5000000 | tf_op jit(solution)/shard_map/raw/pallas_call | solution.py:230
  268.8 4.8 %all-to-all-start.3 = ((f32[8,1,48]{2,1,0:T(1,128)}), f32[8,1,48]{2,1,0:T(1,128)S(1)}, u32[]{:S(2)}, u32[]{:S(2)}) async-start(f32[8,1,48]{2,1,0:T(1,128)} %bitcast.31), calls=%async_computation.5 | async-start | bytes 8192 | tf_op jit(solution)/shard_map/all_to_all | solution.py:312
  273.6 8.1 %fusion.13 = bf16[1024,768]{1,0:T(8,128)(2,1)} fusion(bf16[1024,768]{1,0:T(8,128)(2,1)} %param.12, bf16[1024,1536]{1,0:T(8,128)(2,1)} %copy-done.8, bf16[768,1536]{1,0:T(8,128)(2,1)} %copy-done.3), kind=kOutput, calls=%fused_computation.24 | convolution fusion | flops 2431647744 | bytes 8650752 | tf_op jit(solution)/shard_map/dot_general | solution.py:327
  (93 shorter events, 55.9 us)
Async XLA Ops:
  8.0 71.9 %all-gather.5.cloned.1.call-start = ((), (), s32[]{:S(2)}) async-start(), calls=%async_computation.8 | async-start | bytes 1658880 | tf_op jit(solution)/shard_map/all_gather | solution.py:272
  11.0 26.5 %copy-start.11 = (bf16[1,96,1536]{2,1,0:T(8,128)(2,1)S(1)}, bf16[1,96,1536]{2,1,0:T(8,128)(2,1)}, u32[]{:S(2)}) copy-start(bf16[1,96,1536]{2,1,0:T(8,128)(2,1)} %param.11) | copy-start | bytes 884740
  11.0 26.5 %copy-start.12 = (bf16[24,1536]{1,0:T(8,128)(2,1)S(1)}, bf16[24,1536]{1,0:T(8,128)(2,1)}, u32[]{:S(2)}) copy-start(bf16[24,1536]{1,0:T(8,128)(2,1)} %param.13) | copy-start | bytes 221188
  12.1 26.3 %copy-start.2 = (bf16[1,1,384,3072]{3,2,1,0:T(8,128)(2,1)S(1)}, bf16[1,1,384,3072]{3,2,1,0:T(8,128)(2,1)}, u32[]{:S(2)}) copy-start(bf16[1,1,384,3072]{3,2,1,0:T(8,128)(2,1)} %param.10) | copy-start | bytes 7077892
  37.5 3.9 %collective-permute-start = (bf16[4,136,1536]{2,1,0:T(8,128)(2,1)}, bf16[4,136,1536]{2,1,0:T(8,128)(2,1)}, u32[]{:S(2)}, u32[]{:S(2)}) collective-permute-start(bf16[4,136,1536]{2,1,0:T(8,128)(2,1)} %all_to_all.24.mine), channel_id=1, source_target_pairs={{0,1},{1,0},{2,3},{3,2},{4,5},{5,4},{6,7},{7,6},{8,9},{9,8},{10,11... | collective-permute-start | bytes 5013512 | tf_op jit(solution)/shard_map/ppermute | solution.py:24
  38.3 136.4 %reduce-scatter.3.cloned.1.call-start = ((), (), s32[]{:S(2)}) async-start(), calls=%async_computation.6 | async-start | bytes 7372800 | tf_op jit(solution)/shard_map/reduce_scatter | solution.py:292
  38.4 6.9 %copy-start.13 = (bf16[1024,768]{1,0:T(8,128)(2,1)S(1)}, bf16[1024,768]{1,0:T(8,128)(2,1)}, u32[]{:S(2)}) copy-start(bf16[1024,768]{1,0:T(8,128)(2,1)} %param.12) | copy-start | bytes 4718596
  45.3 3.0 %copy-start.4 = (f32[384,1]{1,0:T(8,128)}, f32[384,1]{1,0:T(8,128)S(1)}, u32[]{:S(2)}) copy-start(f32[384,1]{1,0:T(8,128)S(1)} %get-tuple-element.36.gate.refs_1_.refs_2_) | copy-start | bytes 4612
  60.4 172.7 %all-gather.7.cloned.1.call-start = ((), (), s32[]{:S(2)}) async-start(), calls=%async_computation.9 | async-start | bytes 7372800 | tf_op jit(solution)/shard_map/all_gather | solution.py:273
  82.1 7.5 %collective-permute-start.13 = (bf16[2,120,768]{2,1,0:T(8,128)(2,1)S(1)}, bf16[2,120,768]{2,1,0:T(8,128)(2,1)S(1)}, u32[]{:S(2)}, u32[]{:S(2)}) collective-permute-start(bf16[2,120,768]{2,1,0:T(8,128)(2,1)S(1)} %get-tuple-element.71), channel_id=1, source_target_pairs={{0,224},{32,0},{64,32},{96,64},{128,96},{160,128},{192,160},{224,1... | collective-permute-start | bytes 1105928 | tf_op jit(solution)/shard_map/ppermute | solution.py:24
  83.8 8.7 %collective-permute-start.9 = (bf16[2,120,768]{2,1,0:T(8,128)(2,1)S(1)}, bf16[2,120,768]{2,1,0:T(8,128)(2,1)S(1)}, u32[]{:S(2)}, u32[]{:S(2)}) collective-permute-start(bf16[2,120,768]{2,1,0:T(8,128)(2,1)S(1)} %get-tuple-element.69), channel_id=1, source_target_pairs={{0,32},{32,64},{64,96},{96,128},{128,160},{160,192},{192,224},{224... | collective-permute-start | bytes 1105928 | tf_op jit(solution)/shard_map/ppermute | solution.py:24
  95.5 14.6 %collective-permute-start.10 = (bf16[4,120,768]{2,1,0:T(8,128)(2,1)}, bf16[4,120,768]{2,1,0:T(8,128)(2,1)}, u32[]{:S(2)}, u32[]{:S(2)}) collective-permute-start(bf16[4,120,768]{2,1,0:T(8,128)(2,1)} %pad_maximum_fusion), channel_id=1, source_target_pairs={{0,32},{32,64},{64,96},{96,128},{128,160},{160,192},{192,224},{224... | collective-permute-start | bytes 2211848 | tf_op jit(solution)/shard_map/ppermute | solution.py:24
  95.5 17.0 %copy-start.10 = (bf16[120,768]{1,0:T(8,128)(2,1)S(1)}, bf16[120,768]{1,0:T(8,128)(2,1)}, u32[]{:S(2)}) copy-start(bf16[120,768]{1,0:T(8,128)(2,1)} %get-tuple-element.73) | copy-start | bytes 552964
  97.5 38.1 %collective-permute-start.14 = (bf16[4,120,768]{2,1,0:T(8,128)(2,1)}, bf16[4,120,768]{2,1,0:T(8,128)(2,1)}, u32[]{:S(2)}, u32[]{:S(2)}) collective-permute-start(bf16[4,120,768]{2,1,0:T(8,128)(2,1)} %pad_maximum_fusion.1), channel_id=1, source_target_pairs={{0,224},{32,0},{64,32},{96,64},{128,96},{160,128},{192,160},{224,1... | collective-permute-start | bytes 2211848 | tf_op jit(solution)/shard_map/ppermute | solution.py:24
  112.4 23.2 %collective-permute-start.11 = (bf16[4,120,768]{2,1,0:T(8,128)(2,1)}, bf16[4,120,768]{2,1,0:T(8,128)(2,1)}, u32[]{:S(2)}, u32[]{:S(2)}) collective-permute-start(bf16[4,120,768]{2,1,0:T(8,128)(2,1)} %fusion.25), channel_id=1, source_target_pairs={{0,32},{32,64},{64,96},{96,128},{128,160},{160,192},{192,224},{224... | collective-permute-start | bytes 2211848 | tf_op jit(solution)/shard_map/ppermute | solution.py:24
  113.4 18.9 %all-to-all-start.1 = ((bf16[4,120,768]{2,1,0:T(8,128)(2,1)}), bf16[4,120,768]{2,1,0:T(8,128)(2,1)}, u32[]{:S(2)}, u32[]{:S(2)}) async-start(bf16[4,120,768]{2,1,0:T(8,128)(2,1)} %broadcast_in_dim.46), calls=%async_computation.1 | async-start | bytes 1474560 | tf_op jit(solution)/shard_map/all_to_all | solution.py:259
  117.6 166.2 %reduce-scatter.5.cloned.1.call-start = ((), (), s32[]{:S(2)}) async-start(), calls=%async_computation.7 | async-start | bytes 1658880 | tf_op jit(solution)/shard_map/reduce_scatter | solution.py:293
  132.3 16.8 %collective-permute-start.1 = (bf16[4,120,768]{2,1,0:T(8,128)(2,1)}, bf16[4,120,768]{2,1,0:T(8,128)(2,1)}, u32[]{:S(2)}, u32[]{:S(2)}) collective-permute-start(bf16[4,120,768]{2,1,0:T(8,128)(2,1)} %all-to-all-done.1.refs_0_), channel_id=1, source_target_pairs={{0,32},{32,64},{64,96},{96,128},{128,160},{160,192},{192,224},{224... | collective-permute-start | bytes 2211848 | tf_op jit(solution)/shard_map/ppermute | solution.py:24
  133.8 19.7 %collective-permute-start.5 = (bf16[4,120,768]{2,1,0:T(8,128)(2,1)}, bf16[4,120,768]{2,1,0:T(8,128)(2,1)}, u32[]{:S(2)}, u32[]{:S(2)}) collective-permute-start(bf16[4,120,768]{2,1,0:T(8,128)(2,1)} %all-to-all-done.1.refs_0_), channel_id=1, source_target_pairs={{0,224},{32,0},{64,32},{96,64},{128,96},{160,128},{192,160},{224,1... | collective-permute-start | bytes 2211848 | tf_op jit(solution)/shard_map/ppermute | solution.py:24
  138.9 30.5 %collective-permute-start.15 = (bf16[4,120,768]{2,1,0:T(8,128)(2,1)}, bf16[4,120,768]{2,1,0:T(8,128)(2,1)}, u32[]{:S(2)}, u32[]{:S(2)}) collective-permute-start(bf16[4,120,768]{2,1,0:T(8,128)(2,1)} %get-tuple-element.66), channel_id=1, source_target_pairs={{0,224},{32,0},{64,32},{96,64},{128,96},{160,128},{192,160},{224,1... | collective-permute-start | bytes 2211848 | tf_op jit(solution)/shard_map/ppermute | solution.py:24
  149.1 25.7 %collective-permute-start.2 = (bf16[4,120,768]{2,1,0:T(8,128)(2,1)}, bf16[4,120,768]{2,1,0:T(8,128)(2,1)}, u32[]{:S(2)}, u32[]{:S(2)}) collective-permute-start(bf16[4,120,768]{2,1,0:T(8,128)(2,1)} %collective-permute-done.1.refs_0_), channel_id=1, source_target_pairs={{0,32},{32,64},{64,96},{96,128},{128,160},{160,192},{192,224},{224... | collective-permute-start | bytes 2211848 | tf_op jit(solution)/shard_map/ppermute | solution.py:24
  153.5 31.6 %collective-permute-start.6 = (bf16[4,120,768]{2,1,0:T(8,128)(2,1)}, bf16[4,120,768]{2,1,0:T(8,128)(2,1)}, u32[]{:S(2)}, u32[]{:S(2)}) collective-permute-start(bf16[4,120,768]{2,1,0:T(8,128)(2,1)} %collective-permute-done.5.refs_0_), channel_id=1, source_target_pairs={{0,224},{32,0},{64,32},{96,64},{128,96},{160,128},{192,160},{224,1... | collective-permute-start | bytes 2211848 | tf_op jit(solution)/shard_map/ppermute | solution.py:24
  156.5 31.6 %collective-permute-start.12 = (bf16[4,120,768]{2,1,0:T(8,128)(2,1)}, bf16[4,120,768]{2,1,0:T(8,128)(2,1)}, u32[]{:S(2)}, u32[]{:S(2)}) collective-permute-start(bf16[4,120,768]{2,1,0:T(8,128)(2,1)} %get-tuple-element.65), channel_id=1, source_target_pairs={{0,32},{32,64},{64,96},{96,128},{128,160},{160,192},{192,224},{224... | collective-permute-start | bytes 2211848 | tf_op jit(solution)/shard_map/ppermute | solution.py:24
  171.7 41.5 %collective-permute-start.16 = (bf16[4,120,768]{2,1,0:T(8,128)(2,1)}, bf16[4,120,768]{2,1,0:T(8,128)(2,1)}, u32[]{:S(2)}, u32[]{:S(2)}) collective-permute-start(bf16[4,120,768]{2,1,0:T(8,128)(2,1)} %fusion.24), channel_id=1, source_target_pairs={{0,224},{32,0},{64,32},{96,64},{128,96},{160,128},{192,160},{224,1... | collective-permute-start | bytes 2211848 | tf_op jit(solution)/shard_map/ppermute | solution.py:24
  174.8 45.4 %collective-permute-start.3 = (bf16[4,120,768]{2,1,0:T(8,128)(2,1)}, bf16[4,120,768]{2,1,0:T(8,128)(2,1)}, u32[]{:S(2)}, u32[]{:S(2)}) collective-permute-start(bf16[4,120,768]{2,1,0:T(8,128)(2,1)} %collective-permute-done.2.refs_0_), channel_id=1, source_target_pairs={{0,32},{32,64},{64,96},{96,128},{128,160},{160,192},{192,224},{224... | collective-permute-start | bytes 2211848 | tf_op jit(solution)/shard_map/ppermute | solution.py:24
  185.1 40.5 %collective-permute-start.7 = (bf16[4,120,768]{2,1,0:T(8,128)(2,1)}, bf16[4,120,768]{2,1,0:T(8,128)(2,1)}, u32[]{:S(2)}, u32[]{:S(2)}) collective-permute-start(bf16[4,120,768]{2,1,0:T(8,128)(2,1)} %collective-permute-done.6.refs_0_), channel_id=1, source_target_pairs={{0,224},{32,0},{64,32},{96,64},{128,96},{160,128},{192,160},{224,1... | collective-permute-start | bytes 2211848 | tf_op jit(solution)/shard_map/ppermute | solution.py:24
  215.9 15.2 %all-to-all-start.2 = ((bf16[4,120,768]{2,1,0:T(8,128)(2,1)}), bf16[4,120,768]{2,1,0:T(8,128)(2,1)}, u32[]{:S(2)}, u32[]{:S(2)}) async-start(bf16[4,120,768]{2,1,0:T(8,128)(2,1)} %fusion.28), calls=%async_computation.4 | async-start | bytes 1474560 | tf_op jit(solution)/shard_map/all_to_all | solution.py:300
  221.9 40.9 %collective-permute-start.4 = (bf16[2,120,768]{2,1,0:T(8,128)(2,1)}, bf16[2,120,768]{2,1,0:T(8,128)(2,1)}, u32[]{:S(2)}, u32[]{:S(2)}) collective-permute-start(bf16[2,120,768]{2,1,0:T(8,128)(2,1)} %slice.68), channel_id=1, source_target_pairs={{0,32},{32,64},{64,96},{96,128},{128,160},{160,192},{192,224},{224... | collective-permute-start | bytes 1105928 | tf_op jit(solution)/shard_map/ppermute | solution.py:24
  227.4 35.4 %collective-permute-start.8 = (bf16[2,120,768]{2,1,0:T(8,128)(2,1)}, bf16[2,120,768]{2,1,0:T(8,128)(2,1)}, u32[]{:S(2)}, u32[]{:S(2)}) collective-permute-start(bf16[2,120,768]{2,1,0:T(8,128)(2,1)} %slice.69), channel_id=1, source_target_pairs={{0,224},{32,0},{64,32},{96,64},{128,96},{160,128},{192,160},{224,1... | collective-permute-start | bytes 1105928 | tf_op jit(solution)/shard_map/ppermute | solution.py:24
  236.7 3.9 %copy-start.1 = (bf16[32,120,768]{2,1,0:T(8,128)(2,1)S(1)}, bf16[32,120,768]{2,1,0:T(8,128)(2,1)}, u32[]{:S(2)}) copy-start(bf16[32,120,768]{2,1,0:T(8,128)(2,1)} %all-gather.7.cloned.1.call-done) | copy-start | bytes 17694724
  268.8 13.0 %all-to-all-start.3 = ((f32[8,1,48]{2,1,0:T(1,128)}), f32[8,1,48]{2,1,0:T(1,128)S(1)}, u32[]{:S(2)}, u32[]{:S(2)}) async-start(f32[8,1,48]{2,1,0:T(1,128)} %bitcast.31), calls=%async_computation.5 | async-start | bytes 8192 | tf_op jit(solution)/shard_map/all_to_all | solution.py:312
  273.6 11.1 %copy-start.9 = (f32[120,768]{1,0:T(8,128)S(1)}, f32[120,768]{1,0:T(8,128)}, u32[]{:S(2)}) copy-start(f32[120,768]{1,0:T(8,128)} %convert_reduce_fusion) | copy-start | bytes 1105924
  (6 other events, 13.1 us)
Sparse Core Ops, SparseCore 0:
  38.4 41.3 all-gather.4
  174.8 44.3 reduce-scatter.4
Sparse Core Ops, SparseCore 1:
  60.5 71.0 reduce-scatter.2
  133.2 65.7 all-gather.6
where the time goes:
time: 296 us; the launch traced here: 294 us
  waiting for transfers between devices  117 us (40%)
  Pallas kernels  40.7 us (14%)
  starting transfers between devices  38 us (13%)
  other arithmetic  28.1 us (9%)
  blocking collectives  25.3 us (9%)
  local copies, waits for them, and re-layouts  18 us (6%)
  between operations  15.8 us (5%)
  matrix products  11.3 us (4%)
    ppermute x17, waiting for transfers between devices, hop(): return lax.ppermute(a, axis, [(i, (i + by) % n) for i in range(n)])  82.4 us
    pallas_call x8, Pallas kernels, raw_block(): pl.pallas_call(raw_kernel, name='raw', out_shape=(jax.ShapeDtypeStruct((s...  29.8 us
    all_to_all x1, blocking collectives, to_all(): return lax.all_to_all(many, axis, 0, 0, tiled=True)  25.3 us
    ppermute x17, starting transfers between devices, hop(): return lax.ppermute(a, axis, [(i, (i + by) % n) for i in range(n)])  24.6 us
    all_gather x1, waiting for transfers between devices, body(): a_whole = lax.all_gather(shard[:, :half], 'z')  19.4 us
    all_to_all x1, waiting for transfers between devices, to_all(): return lax.all_to_all(many, axis, 0, 0, tiled=True)  14.7 us
    unnamed x28, local copies, waits for them, and re-layouts  10.1 us
    convert_element_type x4, other arithmetic, added(): return (a.astype(F32) + b.astype(F32)).astype(BF)  10 us
  transfers between devices with their start and end apart: 24, of which 12 were waited for; matrix products, arithmetic and copies ran while one was open for 14% of the time, Pallas kernels for 14%

commit v1 on v0

--- a/solution.py
+++ b/solution.py
@@ -1,3 +1,5 @@
+import functools
+
 import jax
 import jax.numpy as jnp
 from jax import lax
@@ -139,61 +141,78 @@
     out = lax.dot_general(
         hidden[...], scal[...], (((0,), (0,)), ((), ())), preferred_element_type=F32
     )
-    nx, rows, half = tb.shape[1], hidden.shape[1] // tb.shape[1], tb.shape[3]
-    out = out.astype(BF).reshape(nx, rows, 2 * half)
-    ta[:, 0, :rows, :] = out[:, :, :half]
-    tb[0, :, :rows, :] = out[:, :, half:]
-    ta[:, 0, rows:, :] = tsh[0, :, :, :half]
-    tb[0, :, rows:, :] = tsh[0, :, :, half:]
+    nx, half = tb.shape[1], tb.shape[3]
+    rows = hidden.shape[1] // nx
+    out = out.astype(BF).reshape(nx, rows, half)
+
+    @pl.when(pl.program_id(0) == 0)
+    def _():
+        ta[:, 0, :rows, :] = out
+        ta[:, 0, rows:, :] = tsh[0]
+
+    @pl.when(pl.program_id(0) == 1)
+    def _():
+        tb[0, :, :rows, :] = out
+        tb[0, :, rows:, :] = tsh[0]
 
 
 def terms(hidden, scal, tsh):
     slots, hid = hidden.shape
-    width = scal.shape[1]
+    half = scal.shape[1] // 2
     rows, extra = hid // (NZ * NX), tsh.shape[2]
-    tail = (rows + extra, width // 2)
+    tail = (rows + extra, half)
     return pl.pallas_call(
         terms_kernel,
         name="terms",
-        grid=(NZ,),
+        grid=(2, NZ),
         out_shape=(
             jax.ShapeDtypeStruct((NX, NZ, *tail), BF),
             jax.ShapeDtypeStruct((NZ, NX, *tail), BF),
         ),
         in_specs=[
-            pl.BlockSpec((slots, hid // NZ), lambda k: (0, k)),
-            pl.BlockSpec((slots, width), lambda k: (0, 0)),
-            pl.BlockSpec((1, NX, extra, width), lambda k: (k, 0, 0, 0)),
+            pl.BlockSpec((slots, hid // NZ), lambda j, k: (0, k)),
+            pl.BlockSpec((slots, half), lambda j, k: (0, j)),
+            pl.BlockSpec((1, NX, extra, half), lambda j, k: (k, 0, 0, j)),
         ],
         out_specs=(
-            pl.BlockSpec((NX, 1, *tail), lambda k: (0, k, 0, 0)),
-            pl.BlockSpec((1, NX, *tail), lambda k: (k, 0, 0, 0)),
+            pl.BlockSpec((NX, 1, *tail), lambda j, k: (0, k * (1 - j) + (NZ - 1) * j, 0, 0)),
+            pl.BlockSpec((1, NX, *tail), lambda j, k: (k * j, 0, 0, 0)),
         ),
         compiler_params=pltpu.CompilerParams(vmem_limit_bytes=24 << 20),
         cost_estimate=pl.CostEstimate(
-            flops=2 * slots * hid * width, bytes_accessed=18_000_000, transcendentals=0
+            flops=4 * slots * hid * half, bytes_accessed=20_000_000, transcendentals=0
         ),
     )(hidden, scal, tsh)
 
 
 RAW_STEPS = 3
-ARRIVAL = (0, 1, 7, 2, 6, 3, 5, 4)
-
-
-def raw_kernel(sc, rows, gate, pre, a_ref, *refs):
+OFFLOADED = 1152
+GROUPS = ((0, 1, 7), (2, 6), (3, 5), (4,))
+
+
+def raw_kernel(parts, sc, rows, gate, pre, a_ref, *refs):
     *b_refs, _, _, out, wsh, score, whole, small = refs
     n_rows = whole.shape[0] // NX
     extra = small.shape[0] // NX
-    half = whole.shape[1] // 2
-
-    @pl.when(pl.program_id(0) == 0)
+    half = a_ref.shape[3]
+
+    @pl.when(pl.program_id(1) == 0)
     def _():
         for k in range(NX):
-            b_ref, i = (b_refs[0], k) if len(b_refs) == 1 else (b_refs[k // 2], k % 2)
-            whole[k * n_rows : (k + 1) * n_rows, :half] = a_ref[k, 0, :n_rows, :]
-            whole[k * n_rows : (k + 1) * n_rows, half:] = b_ref[i, :n_rows, :]
-            small[k * extra : (k + 1) * extra, :half] = a_ref[k, 0, n_rows:, :].astype(F32)
-            small[k * extra : (k + 1) * extra, half:] = b_ref[i, n_rows:, :].astype(F32)
+            whole[k * n_rows : (k + 1) * n_rows, :half] = a_ref[0, k, :n_rows, :]
+            small[k * extra : (k + 1) * extra, :half] = a_ref[0, k, n_rows:, :].astype(F32)
+        at = 0
+        for p, n in enumerate(parts):
+            mine = b_refs[at : at + n]
+            at += n
+
+            @pl.when(pl.program_id(0) == p)
+            def _():
+                for k in range(NX):
+                    b_ref, i = mine[k * n // NX], k % (NX // n)
+                    whole[k * n_rows : (k + 1) * n_rows, half:] = b_ref[i, :n_rows, :]
+                    small[k * extra : (k + 1) * extra, half:] = b_ref[i, n_rows:, :].astype(F32)
+
         wsh[...] = small[...].astype(BF)
 
     raw = lax.dot_general(
@@ -201,24 +220,25 @@
     )
     value, slope = gelu_pair(pre[...].astype(F32))
     out[...] = (gate[...] * raw * slope).astype(BF)
-    score[...] = jnp.sum(value * raw, axis=1, keepdims=True)
-
-
-def raw_block(scalars, rows, gate, pre, a_whole, b_piece, carried):
+    score[0] = jnp.sum(value * raw, axis=1, keepdims=True)
+
+
+def raw_blocks(scalars, rows, gate, pre, a_whole, b_group, carried):
     slots, width = rows.shape
     hid = pre.shape[1]
     block, step = hid // NZ, slots // RAW_STEPS
     n_rows = block // NX
     extra = a_whole.shape[2] - n_rows
-    half = width // 2
-    b_list = list(b_piece) if isinstance(b_piece, tuple) else [b_piece]
+    b_group = [list(b) if isinstance(b, tuple) else [b] for b in b_group]
+    parts = tuple(len(b) for b in b_group)
+    b_list = sum(b_group, [])
     in_specs = [
-        pl.BlockSpec((step, width), lambda i, sc: (i, 0)),
-        pl.BlockSpec((step, 1), lambda i, sc: (i, 0)),
-        pl.BlockSpec((step, block), lambda i, sc: (i, sc[0])),
-        pl.BlockSpec((NX, 1, n_rows + extra, half), lambda i, sc: (0, sc[0], 0, 0)),
+        pl.BlockSpec((step, width), lambda p, i, sc: (i, 0)),
+        pl.BlockSpec((step, 1), lambda p, i, sc: (i, 0)),
+        pl.BlockSpec((step, block), lambda p, i, sc: (i, sc[p])),
+        pl.BlockSpec((1, *a_whole.shape[1:]), lambda p, i, sc: (sc[p], 0, 0, 0)),
     ]
-    in_specs += [pl.BlockSpec(b.shape, lambda i, sc: (0, 0, 0)) for b in b_list]
+    in_specs += [pl.BlockSpec(b.shape, lambda p, i, sc: (0, 0, 0)) for b in b_list]
     args = [rows, gate, pre, a_whole, *b_list]
     aliases = {}
     in_specs += [pl.BlockSpec(memory_space=pl.ANY)] * 2
@@ -227,29 +247,32 @@
         args += list(carried)
     else:
         args += [gate, gate]
+    n = len(parts)
     return pl.pallas_call(
-        raw_kernel,
+        functools.partial(raw_kernel, parts),
         name="raw",
         out_shape=(
             jax.ShapeDtypeStruct((slots, hid), BF),
             jax.ShapeDtypeStruct((NZ * NX * extra, width), BF),
-            jax.ShapeDtypeStruct((slots, 1), F32),
+            jax.ShapeDtypeStruct((n, slots, 1), F32),
         ),
         grid_spec=pltpu.PrefetchScalarGridSpec(
             num_scalar_prefetch=1,
-            grid=(RAW_STEPS,),
+            grid=(n, RAW_STEPS),
             in_specs=in_specs,
             out_specs=(
-                pl.BlockSpec((step, block), lambda i, sc: (i, sc[0])),
-                pl.BlockSpec((NX * extra, width), lambda i, sc: (sc[0], 0)),
-                pl.BlockSpec((step, 1), lambda i, sc: (i, 0)),
+                pl.BlockSpec((step, block), lambda p, i, sc: (i, sc[p])),
+                pl.BlockSpec((NX * extra, width), lambda p, i, sc: (sc[p], 0)),
+                pl.BlockSpec((1, step, 1), lambda p, i, sc: (p, i, 0)),
             ),
             scratch_shapes=[pltpu.VMEM((block, width), BF), pltpu.VMEM((NX * extra, width), F32)],
         ),
         input_output_aliases=aliases,
         compiler_params=pltpu.CompilerParams(vmem_limit_bytes=16 << 20),
         cost_estimate=pl.CostEstimate(
-            flops=2 * slots * block * width, bytes_accessed=5_000_000, transcendentals=slots * block
+            flops=2 * n * slots * block * width,
+            bytes_accessed=5_000_000 * n,
+            transcendentals=n * slots * block,
         ),
     )(scalars, *args)
 
@@ -260,18 +283,20 @@
 
 
 def body(grad_out, expert_ids, gates, routed_pre, routed_down, shared_pre, shared_down):
-    z, _, y, c = (lax.axis_index(a) for a in ("z", "x", "y", "c"))
+    z, x, y, c = (lax.axis_index(a) for a in ("z", "x", "y", "c"))
     owner = y * NC + c
     n_exp = NY * NC
     tok, width = grad_out.shape
     slots = routed_pre.shape[2]
     cap = slots // n_exp
-    half = width // 2
 
     shard = jnp.concatenate([routed_down[0], shared_down], axis=0)
-    a_whole = lax.all_gather(shard[:, :half], "z")
-    a_whole = lax.all_gather(a_whole, "x")
-    b_pieces = gather_eight(to_all(shard[:, half:], "x", NX), "z", cut_rows)
+    a_whole = lax.all_gather(shard[:, :OFFLOADED], DP)
+    a_whole = a_whole.reshape(NZ, NX, *a_whole.shape[1:])
+    b_shard = shard[:, OFFLOADED:]
+    around = [b_shard] + [hop(b_shard, "x", -k) for k in range(1, NX)]
+    b_all = lax.dynamic_slice_in_dim(jnp.stack(around + around[:-1]), (NX - x) % NX, NX, 0)
+    b_pieces = gather_eight(b_all, "z", cut_rows)
 
     metas = jnp.concatenate([gates.astype(BF).T, expert_ids.astype(BF).T], axis=0)
     metas = jnp.pad(metas, ((0, 8 - metas.shape[0]), (0, width - tok)))
@@ -289,26 +314,28 @@
         shared_b, group_rows, (((0,), (0,)), ((), ())), preferred_element_type=F32
     ).astype(BF)
     ta, tb = terms(hidden_b, scaled, shared_term.reshape(NZ, NX, -1, width))
-    sum_a = lax.psum_scatter(ta.reshape(-1, half), "x", scatter_dimension=0, tiled=True)
-    sum_a = lax.psum_scatter(sum_a, "z", scatter_dimension=0, tiled=True)
-    sum_a = sum_a.astype(F32)
-
-    def along(r):
-        return lax.dynamic_index_in_dim(tb, (z + r) % NZ, 0, keepdims=False)
-
-    sum_b = sum_ring(along, NZ, "z", cut_rows, join_rows).astype(BF)
-    sum_b = lax.all_to_all(sum_b, "x", 0, 0, tiled=True).astype(F32).sum(axis=0)
+
+    def along(t, place, n):
+        return lambda r: lax.dynamic_index_in_dim(t, (place + r) % n, 0, keepdims=False)
+
+    sum_a = sum_ring(along(ta, x, NX), NX, "x", cut_rows, join_rows).astype(BF)
+    sum_b = sum_ring(along(tb, z, NZ), NZ, "z", cut_rows, join_rows).astype(BF)
+    sum_a = lax.all_to_all(sum_a, "z", 0, 0, tiled=True)
+    sum_b = lax.all_to_all(sum_b, "x", 0, 0, tiled=True)
+    sum_a = sum_a.astype(F32).sum(axis=0)
+    sum_b = sum_b.astype(F32).sum(axis=0)
     total = jnp.concatenate([sum_a, sum_b], axis=1)
     rows = routed_down.shape[1]
 
     carried, scores = None, []
-    for j in ARRIVAL:
-        sc = jnp.stack([(z + (NZ - j)) % NZ]).astype(jnp.int32)
-        out, wsh, score = raw_block(sc, recv_rows, gate_col, pre, a_whole, b_pieces[j], carried)
+    for group in GROUPS:
+        sc = jnp.stack([(z + (NZ - j)) % NZ for j in group]).astype(jnp.int32)
+        pieces = [b_pieces[j] for j in group]
+        out, wsh, score = raw_blocks(sc, recv_rows, gate_col, pre, a_whole, pieces, carried)
         carried = (out, wsh)
         scores.append(score)
     routed_pre_grad, whole_shared = carried
-    slot_score = sum(scores[1:], scores[0])
+    slot_score = jnp.concatenate(scores, axis=0).sum(axis=0)
     returned = lax.all_to_all(slot_score.reshape(n_exp, cap), EXPERT, 0, 0, tiled=True)
 
     labels = jnp.arange(n_exp, dtype=jnp.int32)

time: 296 us -> 359 us (1.21)
  local copies, waits for them, and re-layouts: 18 us -> 42.1 us
  other arithmetic: 28.1 us -> 45.4 us
  waiting for transfers between devices: 117 us -> 131 us
  starting transfers between devices: 38 us -> 48.5 us
    ppermute x17 -> x24, waiting for transfers between devices: 82.4 us -> 129 us  [hop(): return lax.ppermute(a, axis, [(i, (i + by) % n) for i in range(n)])]
    unnamed x28 -> x61, local copies, waits for them, and re-layouts: 10.1 us -> 31.1 us
    all_gather x2 -> x1, waiting for transfers between devices: 19.4 us -> 0.01 us  [body(): a_whole = lax.all_gather(shard[:, :OFFLOADED], DP)]
    all_to_all x2, waiting for transfers between devices: 14.7 us -> 1.6 us  [the longest x1 1.59 us: body(): sum_b = lax.all_to_all(sum_b, 'x', 0, 0, tiled=True)]
    ppermute x17 -> x24, starting transfers between devices: 24.6 us -> 34.4 us  [hop(): return lax.ppermute(a, axis, [(i, (i + by) % n) for i in range(n)])]
    reduce_sum x1 -> x7, other arithmetic: 2.01 us -> 7.76 us  [the longest x5 4.12 us: body(): slot_score = jnp.concatenate(scores, axis=0).sum(axis=0)]
    pallas_call x9 -> x5, Pallas kernels: 36.8 us -> 34.5 us  [the longest x4 23.7 us: raw_blocks(): pl.pallas_call(functools.partial(raw_kernel, parts), name='raw', out_shap...]
    slice x3 -> x4, local copies, waits for them, and re-layouts: 5.67 us -> 7.68 us  [cut_rows(): return (a[:half], a[half:])]
  transfers between devices with their start and end apart: 24 -> 28, of which waited for: 12 -> 11; matrix products, arithmetic and copies ran while one was open for 14% -> 20% of each run, Pallas kernels for 14% -> 10%
where the time goes in v1:
time: 359 us; the launch traced here: 356 us
  waiting for transfers between devices  131 us (36%)
  starting transfers between devices  48.5 us (14%)
  other arithmetic  45.4 us (13%)
  local copies, waits for them, and re-layouts  42.1 us (12%)
  Pallas kernels  38.4 us (11%)
  blocking collectives  25.3 us (7%)
  between operations  14.3 us (4%)
  matrix products  11.2 us (3%)
    ppermute x24, waiting for transfers between devices, hop(): return lax.ppermute(a, axis, [(i, (i + by) % n) for i in range(n)])  129 us
    ppermute x24, starting transfers between devices, hop(): return lax.ppermute(a, axis, [(i, (i + by) % n) for i in range(n)])  34.4 us
    unnamed x61, local copies, waits for them, and re-layouts  31.1 us
    all_to_all x1, blocking collectives, to_all(): return lax.all_to_all(many, axis, 0, 0, tiled=True)  25.3 us
    pallas_call x4, Pallas kernels, raw_blocks(): pl.pallas_call(functools.partial(raw_kernel, parts), name='raw', out_shap...  23.7 us
    convert_element_type x5, other arithmetic, added(): return (a.astype(F32) + b.astype(F32)).astype(BF)  11.1 us
    pallas_call x1, Pallas kernels, terms(): pl.pallas_call(terms_kernel, name='terms', grid=(2, NZ), out_shape=(jax.S...  10.9 us
    dot_general x1, matrix products, body(): lax.dot_general(group_rows, whole_shared, (((1,), (1,)), ((), ())), prefe...  8.11 us
  transfers between devices with their start and end apart: 28, of which 11 were waited for; matrix products, arithmetic and copies ran while one was open for 20% of the time, Pallas kernels for 10%

profile of v1, /device:TPU:8, one launch (start us, length us, event | category | flops | bytes accessed | tf_op | source)
XLA Modules:
  0.0 356.2 jit_solution(775266911111373263)
XLA Ops:
  13.6 25.3 %all_to_all.21.mine = bf16[4,136,1536]{2,1,0:T(8,128)(2,1)} all-to-all(bf16[4,136,1536]{2,1,0:T(8,128)(2,1)S(1)} %broadcast_in_dim.39), channel_id=1, replica_groups=mesh['z'=8,'x'=4,'y'=4,'c'=2] {'y'}, dimensions={0} | all-to-all | bytes 3342336 | tf_op jit(solution)/shard_map/all_to_all | solution.py:282
  42.8 3.9 %dispatch.1 = (bf16[1024,1536]{1,0:T(8,128)(2,1)S(1)}, bf16[384,1536]{1,0:T(8,128)(2,1)S(1)}, bf16[384,1536]{1,0:T(8,128)(2,1)S(1)}, f32[384,1]{1,0:T(8,128)S(1)}) custom-call(s32[2]{0:T(128)S(1)} %pad_add_fusion.sc, bf16[4,136,1536]{2,1,0:T(8,128)(2,1)} %all_to_all.21.mine, bf16[4,136,1536]{2,1,0:T(8,128)(2,1)} %collective-permute-done.partner), custom_call_target="tpu_custom_call" | custom-call | flops 200000000 | bytes 10000000 | tf_op jit(solution)/shard_map/dispatch/pallas_call | solution.py:123
  46.7 3.0 convolution_convert_fusion
  49.7 10.9 %terms.1 = (bf16[4,8,120,768]{3,2,1,0:T(8,128)(2,1)S(1)}, bf16[8,4,120,768]{3,2,1,0:T(8,128)(2,1)S(1)}) custom-call(bf16[384,3072]{1,0:T(8,128)(2,1)S(1)} %fusion.1.hidden, bf16[384,1536]{1,0:T(8,128)(2,1)S(1)} %get-tuple-element.32.scal, bf16[8,4,24,1536]{3,2,1,0:T(8,128)(2,1)S(1)} %bitcast.100), custom_call_target="tpu_custom_call" | custom-call | flops 3623878656 | bytes 20000000 | tf_op jit(solution)/shard_map/terms/pallas_call | solution.py:164
  60.6 2.6 copy-done.11
  66.1 3.9 %collective-permute-start.20 = (bf16[2,120,768]{2,1,0:T(8,128)(2,1)S(1)}, bf16[2,120,768]{2,1,0:T(8,128)(2,1)S(1)}, u32[]{:S(2)}, u32[]{:S(2)}) collective-permute-start(bf16[2,120,768]{2,1,0:T(8,128)(2,1)S(1)} %get-tuple-element.49), channel_id=1, source_target_pairs={{0,224},{32,0},{64,32},{96,64},{128,96},{160,128},{192,160},{224,1... | collective-permute-start | bytes 1105928 | tf_op jit(solution)/shard_map/ppermute | solution.py:26
  70.0 17.2 %collective-permute-done.16 = bf16[2,120,768]{2,1,0:T(8,128)(2,1)S(1)} collective-permute-done((bf16[2,120,768]{2,1,0:T(8,128)(2,1)S(1)}, bf16[2,120,768]{2,1,0:T(8,128)(2,1)S(1)}, u32[]{:S(2)}, u32[]{:S(2)}) %collective-permute-start.16) | collective-permute-done | bytes 368672 | tf_op jit(solution)/shard_map/ppermute | solution.py:26
  91.1 3.3 collective-permute-start.21
  94.4 31.1 %collective-permute-done.17 = bf16[4,120,768]{2,1,0:T(8,128)(2,1)} collective-permute-done((bf16[4,120,768]{2,1,0:T(8,128)(2,1)}, bf16[4,120,768]{2,1,0:T(8,128)(2,1)}, u32[]{:S(2)}, u32[]{:S(2)}) %collective-permute-start.17) | collective-permute-done | bytes 737312 | tf_op jit(solution)/shard_map/ppermute | solution.py:26
  127.8 3.5 dynamic-slice_bitcast_fusion.4
  134.5 14.3 %collective-permute-done.18 = bf16[4,120,768]{2,1,0:T(8,128)(2,1)} collective-permute-done((bf16[4,120,768]{2,1,0:T(8,128)(2,1)}, bf16[4,120,768]{2,1,0:T(8,128)(2,1)}, u32[]{:S(2)}, u32[]{:S(2)}) %collective-permute-start.18) | collective-permute-done | bytes 737312 | tf_op jit(solution)/shard_map/ppermute | solution.py:26
  148.8 3.2 fusion.28
  162.0 8.2 %collective-permute-done.22 = bf16[4,120,768]{2,1,0:T(8,128)(2,1)} collective-permute-done((bf16[4,120,768]{2,1,0:T(8,128)(2,1)}, bf16[4,120,768]{2,1,0:T(8,128)(2,1)}, u32[]{:S(2)}, u32[]{:S(2)}) %collective-permute-start.22) | collective-permute-done | bytes 737312 | tf_op jit(solution)/shard_map/ppermute | solution.py:26
  175.0 4.8 %collective-permute-done.19 = bf16[4,120,768]{2,1,0:T(8,128)(2,1)} collective-permute-done((bf16[4,120,768]{2,1,0:T(8,128)(2,1)}, bf16[4,120,768]{2,1,0:T(8,128)(2,1)}, u32[]{:S(2)}, u32[]{:S(2)}) %collective-permute-start.19) | collective-permute-done | bytes 737312 | tf_op jit(solution)/shard_map/ppermute | solution.py:26
  179.8 10.2 %collective-permute-done.23 = bf16[4,120,768]{2,1,0:T(8,128)(2,1)} collective-permute-done((bf16[4,120,768]{2,1,0:T(8,128)(2,1)}, bf16[4,120,768]{2,1,0:T(8,128)(2,1)}, u32[]{:S(2)}, u32[]{:S(2)}) %collective-permute-start.23) | collective-permute-done | bytes 737312 | tf_op jit(solution)/shard_map/ppermute | solution.py:26
  190.0 2.7 fusion.30
  192.7 4.2 %all-to-all-start.2 = ((bf16[4,120,768]{2,1,0:T(8,128)(2,1)}), bf16[4,120,768]{2,1,0:T(8,128)(2,1)}, u32[]{:S(2)}, u32[]{:S(2)}) async-start(bf16[4,120,768]{2,1,0:T(8,128)(2,1)} %fusion.30), calls=%async_computation.2 | async-start | bytes 1474560 | tf_op jit(solution)/shard_map/all_to_all | solution.py:324
  198.5 3.2 collective-permute-start.1
  203.4 3.9 %fusion.19 = bf16[8,120,768]{2,1,0:T(8,128)(2,1)} fusion(bf16[8,120,768]{2,1,0:T(8,128)(2,1)} %collective-permute-done.15, bf16[8,120,768]{2,1,0:T(8,128)(2,1)} %collective-permute-done.13, bf16[4,8,120,768]{3,2,1,0:T(8,128)(2,1)} %copy-done.11, s32[]{:T(128)S(6)} %select_n.133), kind=kLoop, calls=%fused_computation.31 | loop fusion | flops 4423680 | bytes 5898244 | tf_op jit(solution)/shard_map/convert_element_type | solution.py:321
  208.9 4.5 %all-to-all-start.1 = ((bf16[8,120,768]{2,1,0:T(8,128)(2,1)}), bf16[8,120,768]{2,1,0:T(8,128)(2,1)}, u32[]{:S(2)}, u32[]{:S(2)}) async-start(bf16[8,120,768]{2,1,0:T(8,128)(2,1)} %fusion.19), calls=%async_computation.1 | async-start | bytes 2949120 | tf_op jit(solution)/shard_map/all_to_all | solution.py:323
  223.7 3.3 collective-permute-start.8
  227.8 26.0 %collective-permute-done.8.refs_2_ = bf16[4,120,384]{2,1,0:T(8,128)(2,1)S(1)} collective-permute-done((bf16[4,120,384]{2,1,0:T(8,128)(2,1)S(1)}, bf16[4,120,384]{2,1,0:T(8,128)(2,1)S(1)}, u32[]{:S(2)}, u32[]{:S(2)}) %collective-permute-start.8) | collective-permute-done | bytes 368672 | tf_op jit(solution)/shard_map/ppermute | solution.py:26
  257.3 7.9 %collective-permute-done.9.refs_1_ = bf16[4,120,384]{2,1,0:T(8,128)(2,1)} collective-permute-done((bf16[4,120,384]{2,1,0:T(8,128)(2,1)S(1)}, bf16[4,120,384]{2,1,0:T(8,128)(2,1)}, u32[]{:S(2)}, u32[]{:S(2)}) %collective-permute-start.9) | collective-permute-done | bytes 368672 | tf_op jit(solution)/shard_map/ppermute | solution.py:26
  267.4 7.5 %collective-permute-done.10.refs_1_ = bf16[4,120,384]{2,1,0:T(8,128)(2,1)} collective-permute-done((bf16[4,120,384]{2,1,0:T(8,128)(2,1)}, bf16[4,120,384]{2,1,0:T(8,128)(2,1)}, u32[]{:S(2)}, u32[]{:S(2)}) %collective-permute-start.10) | collective-permute-done | bytes 368672 | tf_op jit(solution)/shard_map/ppermute | solution.py:26
  286.3 3.5 copy-done
  293.7 7.3 %raw.4 = (bf16[384,3072]{1,0:T(8,128)(2,1)}, bf16[768,1536]{1,0:T(8,128)(2,1)S(1)}, f32[3,384,1]{2,1,0:T(8,128)S(1)}) custom-call(s32[3]{0:T(128)S(1)} %pad_add_fusion.3.sc, bf16[384,1536]{1,0:T(8,128)(2,1)S(1)} %get-tuple-element.23.rows, f32[384,1]{1,0:T(8,128)S(1)} %copy-done.8, bf16[384,3072]{1,0:T(8,128)(2,1)S(1)} %bitcast.96, ...), custom_call_target="tpu_custom_call" | custom-call | flops 1358954496 | bytes 15000000 | tf_op jit(solution)/shard_map/raw/pallas_call | solution.py:251
  301.1 6.4 %raw.5 = (bf16[384,3072]{1,0:T(8,128)(2,1)}, bf16[768,1536]{1,0:T(8,128)(2,1)S(1)}, f32[2,384,1]{2,1,0:T(8,128)S(1)}) custom-call(s32[2]{0:T(128)S(1)} %pad_add_fusion.2.sc, bf16[384,1536]{1,0:T(8,128)(2,1)S(1)} %get-tuple-element.23.rows, f32[384,1]{1,0:T(8,128)S(1)} %copy-done.8, ...), custom_call_target="tpu_custom_call", output_to_operand_aliasing={{0}: (7, {}), {1}: (8, {})} | custom-call | flops 905969664 | bytes 10000000 | tf_op jit(solution)/shard_map/raw/pallas_call | solution.py:251
  308.2 6.4 %raw.6 = (bf16[384,3072]{1,0:T(8,128)(2,1)}, bf16[768,1536]{1,0:T(8,128)(2,1)S(1)}, f32[2,384,1]{2,1,0:T(8,128)S(1)}) custom-call(s32[2]{0:T(128)S(1)} %pad_add_fusion.1.sc, bf16[384,1536]{1,0:T(8,128)(2,1)S(1)} %get-tuple-element.23.rows, f32[384,1]{1,0:T(8,128)S(1)} %copy-done.8, ...), custom_call_target="tpu_custom_call", output_to_operand_aliasing={{0}: (7, {}), {1}: (8, {})} | custom-call | flops 905969664 | bytes 10000000 | tf_op jit(solution)/shard_map/raw/pallas_call | solution.py:251
  320.4 3.5 copy-done.2
  326.5 3.6 %raw.7 = (bf16[384,3072]{1,0:T(8,128)(2,1)}, bf16[768,1536]{1,0:T(8,128)(2,1)S(1)}, f32[1,384,1]{2,1,0:T(8,128)S(1)}) custom-call(s32[1]{0:T(128)} %bitcast.sc, bf16[384,1536]{1,0:T(8,128)(2,1)S(1)} %get-tuple-element.23.rows, f32[384,1]{1,0:T(8,128)S(1)} %copy-done.9, bf16[384,3072]{1,0:T(8,128)(2,1)S(1)} %bitcast.99, ...), custom_call_target="tpu_custom_call", output_to_operand_aliasing={{0}: (7, {}), {1}: (8, {})} | custom-call | flops 452984832 | bytes 5000000 | tf_op jit(solution)/shard_map/raw/pallas_call | solution.py:251
  333.9 5.4 %all-to-all-start.3 = ((f32[8,1,48]{2,1,0:T(1,128)}), f32[8,1,48]{2,1,0:T(1,128)S(1)}, u32[]{:S(2)}, u32[]{:S(2)}) async-start(f32[8,1,48]{2,1,0:T(1,128)} %bitcast.40), calls=%async_computation.3 | async-start | bytes 8192 | tf_op jit(solution)/shard_map/all_to_all | solution.py:339
  339.3 8.1 %fusion.13 = bf16[1024,768]{1,0:T(8,128)(2,1)} fusion(bf16[1024,768]{1,0:T(8,128)(2,1)} %param.12, bf16[1024,1536]{1,0:T(8,128)(2,1)} %copy-done.22, bf16[768,1536]{1,0:T(8,128)(2,1)} %copy-done.6), kind=kOutput, calls=%fused_computation.24 | convolution fusion | flops 2431647744 | bytes 8650752 | tf_op jit(solution)/shard_map/dot_general | solution.py:354
  (143 shorter events, 89.3 us)
Async XLA Ops:
  7.2 279.2 %all-gather.3.cloned.1.call-start = ((), (), s32[]{:S(2)}) async-start(), calls=%async_computation.4 | async-start | bytes 9123840 | tf_op jit(solution)/shard_map/all_gather | solution.py:294
  13.5 25.5 %copy-start.3 = (bf16[1,1,384,3072]{3,2,1,0:T(8,128)(2,1)S(1)}, bf16[1,1,384,3072]{3,2,1,0:T(8,128)(2,1)}, u32[]{:S(2)}) copy-start(bf16[1,1,384,3072]{3,2,1,0:T(8,128)(2,1)} %param.10) | copy-start | bytes 7077892
  38.9 3.9 %collective-permute-start = (bf16[4,136,1536]{2,1,0:T(8,128)(2,1)}, bf16[4,136,1536]{2,1,0:T(8,128)(2,1)}, u32[]{:S(2)}, u32[]{:S(2)}) collective-permute-start(bf16[4,136,1536]{2,1,0:T(8,128)(2,1)} %all_to_all.21.mine), channel_id=1, source_target_pairs={{0,1},{1,0},{2,3},{3,2},{4,5},{5,4},{6,7},{7,6},{8,9},{9,8},{10,11... | collective-permute-start | bytes 5013512 | tf_op jit(solution)/shard_map/ppermute | solution.py:26
  39.0 7.7 %copy-start.27 = (bf16[1024,768]{1,0:T(8,128)(2,1)S(1)}, bf16[1024,768]{1,0:T(8,128)(2,1)}, u32[]{:S(2)}) copy-start(bf16[1024,768]{1,0:T(8,128)(2,1)} %param.12) | copy-start | bytes 4718596
  63.2 25.9 %copy-start.10 = (bf16[8,4,120,768]{3,2,1,0:T(8,128)(2,1)}, bf16[8,4,120,768]{3,2,1,0:T(8,128)(2,1)S(1)}, u32[]{:S(2)}) copy-start(bf16[8,4,120,768]{3,2,1,0:T(8,128)(2,1)S(1)} %get-tuple-element.35) | copy-start | bytes 17694724
  64.2 23.1 %collective-permute-start.16 = (bf16[2,120,768]{2,1,0:T(8,128)(2,1)S(1)}, bf16[2,120,768]{2,1,0:T(8,128)(2,1)S(1)}, u32[]{:S(2)}, u32[]{:S(2)}) collective-permute-start(bf16[2,120,768]{2,1,0:T(8,128)(2,1)S(1)} %get-tuple-element.47), channel_id=1, source_target_pairs={{0,32},{32,64},{64,96},{96,128},{128,160},{160,192},{192,224},{224... | collective-permute-start | bytes 1105928 | tf_op jit(solution)/shard_map/ppermute | solution.py:26
  66.1 21.1 %collective-permute-start.20 = (bf16[2,120,768]{2,1,0:T(8,128)(2,1)S(1)}, bf16[2,120,768]{2,1,0:T(8,128)(2,1)S(1)}, u32[]{:S(2)}, u32[]{:S(2)}) collective-permute-start(bf16[2,120,768]{2,1,0:T(8,128)(2,1)S(1)} %get-tuple-element.49), channel_id=1, source_target_pairs={{0,224},{32,0},{64,32},{96,64},{128,96},{160,128},{192,160},{224,1... | collective-permute-start | bytes 1105928 | tf_op jit(solution)/shard_map/ppermute | solution.py:26
  89.1 36.3 %collective-permute-start.17 = (bf16[4,120,768]{2,1,0:T(8,128)(2,1)}, bf16[4,120,768]{2,1,0:T(8,128)(2,1)}, u32[]{:S(2)}, u32[]{:S(2)}) collective-permute-start(bf16[4,120,768]{2,1,0:T(8,128)(2,1)} %pad_maximum_fusion.2), channel_id=1, source_target_pairs={{0,32},{32,64},{64,96},{96,128},{128,160},{160,192},{192,224},{224... | collective-permute-start | bytes 2211848 | tf_op jit(solution)/shard_map/ppermute | solution.py:26
  91.1 43.4 %collective-permute-start.21 = (bf16[4,120,768]{2,1,0:T(8,128)(2,1)}, bf16[4,120,768]{2,1,0:T(8,128)(2,1)}, u32[]{:S(2)}, u32[]{:S(2)}) collective-permute-start(bf16[4,120,768]{2,1,0:T(8,128)(2,1)} %pad_maximum_fusion.3), channel_id=1, source_target_pairs={{0,224},{32,0},{64,32},{96,64},{128,96},{160,128},{192,160},{224,1... | collective-permute-start | bytes 2211848 | tf_op jit(solution)/shard_map/ppermute | solution.py:26
  127.8 21.0 %collective-permute-start.18 = (bf16[4,120,768]{2,1,0:T(8,128)(2,1)}, bf16[4,120,768]{2,1,0:T(8,128)(2,1)}, u32[]{:S(2)}, u32[]{:S(2)}) collective-permute-start(bf16[4,120,768]{2,1,0:T(8,128)(2,1)} %fusion.27), channel_id=1, source_target_pairs={{0,32},{32,64},{64,96},{96,128},{128,160},{160,192},{192,224},{224... | collective-permute-start | bytes 2211848 | tf_op jit(solution)/shard_map/ppermute | solution.py:26
  131.3 22.1 %collective-permute-start.12 = (bf16[4,120,768]{2,1,0:T(8,128)(2,1)}, bf16[4,120,768]{2,1,0:T(8,128)(2,1)}, u32[]{:S(2)}, u32[]{:S(2)}) collective-permute-start(bf16[4,120,768]{2,1,0:T(8,128)(2,1)} %get-tuple-element.53), channel_id=1, source_target_pairs={{0,8},{8,16},{16,24},{24,0},{1,9},{9,17},{17,25},{25,1},{2,10},{10... | collective-permute-start | bytes 2211848 | tf_op jit(solution)/shard_map/ppermute | solution.py:26
  132.7 20.6 %collective-permute-start.14 = (bf16[4,120,768]{2,1,0:T(8,128)(2,1)}, bf16[4,120,768]{2,1,0:T(8,128)(2,1)}, u32[]{:S(2)}, u32[]{:S(2)}) collective-permute-start(bf16[4,120,768]{2,1,0:T(8,128)(2,1)} %get-tuple-element.55), channel_id=1, source_target_pairs={{0,24},{8,0},{16,8},{24,16},{1,25},{9,1},{17,9},{25,17},{2,26},{10... | collective-permute-start | bytes 2211848 | tf_op jit(solution)/shard_map/ppermute | solution.py:26
  152.0 18.2 %collective-permute-start.22 = (bf16[4,120,768]{2,1,0:T(8,128)(2,1)}, bf16[4,120,768]{2,1,0:T(8,128)(2,1)}, u32[]{:S(2)}, u32[]{:S(2)}) collective-permute-start(bf16[4,120,768]{2,1,0:T(8,128)(2,1)} %get-tuple-element.44), channel_id=1, source_target_pairs={{0,224},{32,0},{64,32},{96,64},{128,96},{160,128},{192,160},{224,1... | collective-permute-start | bytes 2211848 | tf_op jit(solution)/shard_map/ppermute | solution.py:26
  156.9 46.6 %collective-permute-start.13 = (bf16[8,120,768]{2,1,0:T(8,128)(2,1)}, bf16[8,120,768]{2,1,0:T(8,128)(2,1)}, u32[]{:S(2)}, u32[]{:S(2)}) collective-permute-start(bf16[8,120,768]{2,1,0:T(8,128)(2,1)} %pad_maximum_fusion), channel_id=1, source_target_pairs={{0,8},{8,16},{16,24},{24,0},{1,9},{9,17},{17,25},{25,1},{2,10},{10... | collective-permute-start | bytes 4423688 | tf_op jit(solution)/shard_map/ppermute | solution.py:26
  159.6 43.9 %collective-permute-start.15 = (bf16[8,120,768]{2,1,0:T(8,128)(2,1)}, bf16[8,120,768]{2,1,0:T(8,128)(2,1)}, u32[]{:S(2)}, u32[]{:S(2)}) collective-permute-start(bf16[8,120,768]{2,1,0:T(8,128)(2,1)} %pad_maximum_fusion.1), channel_id=1, source_target_pairs={{0,24},{8,0},{16,8},{24,16},{1,25},{9,1},{17,9},{25,17},{2,26},{10... | collective-permute-start | bytes 4423688 | tf_op jit(solution)/shard_map/ppermute | solution.py:26
  161.4 18.4 %collective-permute-start.19 = (bf16[4,120,768]{2,1,0:T(8,128)(2,1)}, bf16[4,120,768]{2,1,0:T(8,128)(2,1)}, u32[]{:S(2)}, u32[]{:S(2)}) collective-permute-start(bf16[4,120,768]{2,1,0:T(8,128)(2,1)} %get-tuple-element.43), channel_id=1, source_target_pairs={{0,32},{32,64},{64,96},{96,128},{128,160},{160,192},{192,224},{224... | collective-permute-start | bytes 2211848 | tf_op jit(solution)/shard_map/ppermute | solution.py:26
  172.6 17.4 %collective-permute-start.23 = (bf16[4,120,768]{2,1,0:T(8,128)(2,1)}, bf16[4,120,768]{2,1,0:T(8,128)(2,1)}, u32[]{:S(2)}, u32[]{:S(2)}) collective-permute-start(bf16[4,120,768]{2,1,0:T(8,128)(2,1)} %fusion.26), channel_id=1, source_target_pairs={{0,224},{32,0},{64,32},{96,64},{128,96},{160,128},{192,160},{224,1... | collective-permute-start | bytes 2211848 | tf_op jit(solution)/shard_map/ppermute | solution.py:26
  192.7 16.2 %all-to-all-start.2 = ((bf16[4,120,768]{2,1,0:T(8,128)(2,1)}), bf16[4,120,768]{2,1,0:T(8,128)(2,1)}, u32[]{:S(2)}, u32[]{:S(2)}) async-start(bf16[4,120,768]{2,1,0:T(8,128)(2,1)} %fusion.30), calls=%async_computation.2 | async-start | bytes 1474560 | tf_op jit(solution)/shard_map/all_to_all | solution.py:324
  198.5 15.0 %collective-permute-start.1 = (bf16[120,384]{1,0:T(8,128)(2,1)}, bf16[120,384]{1,0:T(8,128)(2,1)}, u32[]{:S(2)}, u32[]{:S(2)}) collective-permute-start(bf16[120,384]{1,0:T(8,128)(2,1)} %get-tuple-element.42), channel_id=1, source_target_pairs={{0,24},{8,0},{16,8},{24,16},{1,25},{9,1},{17,9},{25,17},{2,26},{10... | collective-permute-start | bytes 276488 | tf_op jit(solution)/shard_map/ppermute | solution.py:26
  201.7 13.3 %collective-permute-start.2 = (bf16[120,384]{1,0:T(8,128)(2,1)}, bf16[120,384]{1,0:T(8,128)(2,1)}, u32[]{:S(2)}, u32[]{:S(2)}) collective-permute-start(bf16[120,384]{1,0:T(8,128)(2,1)} %get-tuple-element.42), channel_id=1, source_target_pairs={{0,16},{8,24},{16,0},{24,8},{1,17},{9,25},{17,1},{25,9},{2,18},{10... | collective-permute-start | bytes 276488 | tf_op jit(solution)/shard_map/ppermute | solution.py:26
  202.6 14.0 %collective-permute-start.3 = (bf16[120,384]{1,0:T(8,128)(2,1)}, bf16[120,384]{1,0:T(8,128)(2,1)}, u32[]{:S(2)}, u32[]{:S(2)}) collective-permute-start(bf16[120,384]{1,0:T(8,128)(2,1)} %get-tuple-element.42), channel_id=1, source_target_pairs={{0,8},{8,16},{16,24},{24,0},{1,9},{9,17},{17,25},{25,1},{2,10},{10... | collective-permute-start | bytes 276488 | tf_op jit(solution)/shard_map/ppermute | solution.py:26
  208.9 73.3 %all-to-all-start.1 = ((bf16[8,120,768]{2,1,0:T(8,128)(2,1)}), bf16[8,120,768]{2,1,0:T(8,128)(2,1)}, u32[]{:S(2)}, u32[]{:S(2)}) async-start(bf16[8,120,768]{2,1,0:T(8,128)(2,1)} %fusion.19), calls=%async_computation.1 | async-start | bytes 2949120 | tf_op jit(solution)/shard_map/all_to_all | solution.py:323
  223.7 30.1 %collective-permute-start.8 = (bf16[4,120,384]{2,1,0:T(8,128)(2,1)S(1)}, bf16[4,120,384]{2,1,0:T(8,128)(2,1)S(1)}, u32[]{:S(2)}, u32[]{:S(2)}) collective-permute-start(bf16[4,120,384]{2,1,0:T(8,128)(2,1)S(1)} %constant_dynamic-slice_fusion.refs_0_), channel_id=1, source_target_pairs={{0,224},{32,0},{64,32},{96,64},{128,96},{160,128},{192,160},{224,1... | collective-permute-start | bytes 1105928 | tf_op jit(solution)/shard_map/ppermute | solution.py:26
  227.0 27.5 %collective-permute-start.4 = (bf16[4,120,384]{2,1,0:T(8,128)(2,1)S(1)}, bf16[4,120,384]{2,1,0:T(8,128)(2,1)S(1)}, u32[]{:S(2)}, u32[]{:S(2)}) collective-permute-start(bf16[4,120,384]{2,1,0:T(8,128)(2,1)S(1)} %constant_dynamic-slice_fusion.refs_0_), channel_id=1, source_target_pairs={{0,32},{32,64},{64,96},{96,128},{128,160},{160,192},{192,224},{224... | collective-permute-start | bytes 1105928 | tf_op jit(solution)/shard_map/ppermute | solution.py:26
  253.8 11.4 %collective-permute-start.9 = (bf16[4,120,384]{2,1,0:T(8,128)(2,1)S(1)}, bf16[4,120,384]{2,1,0:T(8,128)(2,1)}, u32[]{:S(2)}, u32[]{:S(2)}) collective-permute-start(bf16[4,120,384]{2,1,0:T(8,128)(2,1)S(1)} %collective-permute-done.8.refs_2_), channel_id=1, source_target_pairs={{0,224},{32,0},{64,32},{96,64},{128,96},{160,128},{192,160},{224,1... | collective-permute-start | bytes 1105928 | tf_op jit(solution)/shard_map/ppermute | solution.py:26
  254.5 10.7 %collective-permute-start.5 = (bf16[4,120,384]{2,1,0:T(8,128)(2,1)S(1)}, bf16[4,120,384]{2,1,0:T(8,128)(2,1)}, u32[]{:S(2)}, u32[]{:S(2)}) collective-permute-start(bf16[4,120,384]{2,1,0:T(8,128)(2,1)S(1)} %collective-permute-done.4.refs_1_), channel_id=1, source_target_pairs={{0,32},{32,64},{64,96},{96,128},{128,160},{160,192},{192,224},{224... | collective-permute-start | bytes 1105928 | tf_op jit(solution)/shard_map/ppermute | solution.py:26
  265.2 9.8 %collective-permute-start.10 = (bf16[4,120,384]{2,1,0:T(8,128)(2,1)}, bf16[4,120,384]{2,1,0:T(8,128)(2,1)}, u32[]{:S(2)}, u32[]{:S(2)}) collective-permute-start(bf16[4,120,384]{2,1,0:T(8,128)(2,1)} %collective-permute-done.9.refs_1_), channel_id=1, source_target_pairs={{0,224},{32,0},{64,32},{96,64},{128,96},{160,128},{192,160},{224,1... | collective-permute-start | bytes 1105928 | tf_op jit(solution)/shard_map/ppermute | solution.py:26
  265.2 12.6 %collective-permute-start.6 = (bf16[4,120,384]{2,1,0:T(8,128)(2,1)}, bf16[4,120,384]{2,1,0:T(8,128)(2,1)}, u32[]{:S(2)}, u32[]{:S(2)}) collective-permute-start(bf16[4,120,384]{2,1,0:T(8,128)(2,1)} %collective-permute-done.5.refs_0_), channel_id=1, source_target_pairs={{0,32},{32,64},{64,96},{96,128},{128,160},{160,192},{192,224},{224... | collective-permute-start | bytes 1105928 | tf_op jit(solution)/shard_map/ppermute | solution.py:26
  276.6 43.7 %collective-permute-start.11 = (bf16[2,120,384]{2,1,0:T(8,128)(2,1)}, bf16[2,120,384]{2,1,0:T(8,128)(2,1)}, u32[]{:S(2)}, u32[]{:S(2)}) collective-permute-start(bf16[2,120,384]{2,1,0:T(8,128)(2,1)} %slice.111), channel_id=1, source_target_pairs={{0,224},{32,0},{64,32},{96,64},{128,96},{160,128},{192,160},{224,1... | collective-permute-start | bytes 552968 | tf_op jit(solution)/shard_map/ppermute | solution.py:26
  279.4 40.9 %collective-permute-start.7 = (bf16[2,120,384]{2,1,0:T(8,128)(2,1)}, bf16[2,120,384]{2,1,0:T(8,128)(2,1)}, u32[]{:S(2)}, u32[]{:S(2)}) collective-permute-start(bf16[2,120,384]{2,1,0:T(8,128)(2,1)} %slice.110), channel_id=1, source_target_pairs={{0,32},{32,64},{64,96},{96,128},{128,160},{160,192},{192,224},{224... | collective-permute-start | bytes 552968 | tf_op jit(solution)/shard_map/ppermute | solution.py:26
  333.9 13.5 %all-to-all-start.3 = ((f32[8,1,48]{2,1,0:T(1,128)}), f32[8,1,48]{2,1,0:T(1,128)S(1)}, u32[]{:S(2)}, u32[]{:S(2)}) async-start(f32[8,1,48]{2,1,0:T(1,128)} %bitcast.40), calls=%async_computation.3 | async-start | bytes 8192 | tf_op jit(solution)/shard_map/all_to_all | solution.py:339
  339.3 9.4 %copy-start.26 = (s32[128,2]{0,1:T(2,128)S(1)}, s32[128,2]{0,1:T(2,128)}, u32[]{:S(2)}) copy-start(s32[128,2]{0,1:T(2,128)} %get-tuple-element.57) | copy-start | bytes 3076
  (24 other events, 53.6 us)
Sparse Core Ops, SparseCore 0:
  10.6 124.6 all-gather.2

commit v2 on v1

--- a/solution.py
+++ b/solution.py
@@ -55,27 +55,21 @@
     return a[:half], a[half:]
 
 
-def sum_ring(block, n, axis, cut, join):
-    far_first, far_second = cut(block(n // 2))
-    right = hop(far_first, axis, 1)
-    left = hop(far_second, axis, -1)
-    for r in range(n // 2 - 1, 0, -1):
-        mine_r, mine_l = block(r), block(n - r)
-        if r == n // 2 - 1:
-            a, b = cut(mine_r)
-            send_r = join(added(a, right), b)
-            a, b = cut(mine_l)
-            send_l = join(a, added(b, left))
-        else:
-            send_r = added(mine_r, right)
-            send_l = added(mine_l, left)
-        right = hop(send_r, axis, 1)
-        left = hop(send_l, axis, -1)
+def sum_ring(block, n, axis):
+    far = block(n // 2)
+    half = far.shape[0] // 2
+    right = hop(far[:half], axis, 1)
+    left = hop(far[half:], axis, -1)
+    rest = ((0, 0),) * (far.ndim - 1)
+    for k, r in enumerate(range(n // 2 - 1, 0, -1)):
+        right, left = lax.optimization_barrier((right, left))
+        if k == 0:
+            right = jnp.pad(right, ((0, half), *rest))
+            left = jnp.pad(left, ((half, 0), *rest))
+        right = hop(added(block(r), right), axis, 1)
+        left = hop(added(block(n - r), left), axis, -1)
+    right, left = lax.optimization_barrier((right, left))
     return block(0).astype(F32) + right.astype(F32) + left.astype(F32)
-
-
-def join_rows(a, b):
-    return jnp.concatenate([a, b], axis=0)
 
 
 def dispatch_kernel(sc, mine, partner, grp, recv, scal, gate):
@@ -141,16 +135,16 @@
     out = lax.dot_general(
         hidden[...], scal[...], (((0,), (0,)), ((), ())), preferred_element_type=F32
     )
-    nx, half = tb.shape[1], tb.shape[3]
+    nx, part = tb.shape[1], tb.shape[3]
     rows = hidden.shape[1] // nx
-    out = out.astype(BF).reshape(nx, rows, half)
+    out = out.astype(BF).reshape(nx, rows, part)
 
     @pl.when(pl.program_id(0) == 0)
     def _():
         ta[:, 0, :rows, :] = out
         ta[:, 0, rows:, :] = tsh[0]
 
-    @pl.when(pl.program_id(0) == 1)
+    @pl.when(pl.program_id(0) > 0)
     def _():
         tb[0, :, :rows, :] = out
         tb[0, :, rows:, :] = tsh[0]
@@ -158,40 +152,46 @@
 
 def terms(hidden, scal, tsh):
     slots, hid = hidden.shape
-    half = scal.shape[1] // 2
+    width = scal.shape[1]
+    part = SUMS_OFFLOADED
     rows, extra = hid // (NZ * NX), tsh.shape[2]
-    tail = (rows + extra, half)
+    high = rows + extra
     return pl.pallas_call(
         terms_kernel,
         name="terms",
-        grid=(2, NZ),
+        grid=(width // part, NZ),
         out_shape=(
-            jax.ShapeDtypeStruct((NX, NZ, *tail), BF),
-            jax.ShapeDtypeStruct((NZ, NX, *tail), BF),
+            jax.ShapeDtypeStruct((NX, NZ, high, part), BF),
+            jax.ShapeDtypeStruct((NZ, NX, high, width - part), BF),
         ),
         in_specs=[
             pl.BlockSpec((slots, hid // NZ), lambda j, k: (0, k)),
-            pl.BlockSpec((slots, half), lambda j, k: (0, j)),
-            pl.BlockSpec((1, NX, extra, half), lambda j, k: (k, 0, 0, j)),
+            pl.BlockSpec((slots, part), lambda j, k: (0, j)),
+            pl.BlockSpec((1, NX, extra, part), lambda j, k: (k, 0, 0, j)),
         ],
         out_specs=(
-            pl.BlockSpec((NX, 1, *tail), lambda j, k: (0, k * (1 - j) + (NZ - 1) * j, 0, 0)),
-            pl.BlockSpec((1, NX, *tail), lambda j, k: (k * j, 0, 0, 0)),
+            pl.BlockSpec(
+                (NX, 1, high, part), lambda j, k: (0, jnp.where(j == 0, k, NZ - 1), 0, 0)
+            ),
+            pl.BlockSpec(
+                (1, NX, high, part),
+                lambda j, k: (jnp.where(j == 0, 0, k), 0, 0, jnp.maximum(j - 1, 0)),
+            ),
         ),
         compiler_params=pltpu.CompilerParams(vmem_limit_bytes=24 << 20),
         cost_estimate=pl.CostEstimate(
-            flops=4 * slots * hid * half, bytes_accessed=20_000_000, transcendentals=0
+            flops=2 * slots * hid * width, bytes_accessed=20_000_000, transcendentals=0
         ),
     )(hidden, scal, tsh)
 
 
 RAW_STEPS = 3
-OFFLOADED = 1152
-GROUPS = ((0, 1, 7), (2, 6), (3, 5), (4,))
+GATHER_OFFLOADED = 896
+SUMS_OFFLOADED = 512
 
 
 def raw_kernel(parts, sc, rows, gate, pre, a_ref, *refs):
-    *b_refs, _, _, out, wsh, score, whole, small = refs
+    *b_refs, out, wsh, score, whole, small = refs
     n_rows = whole.shape[0] // NX
     extra = small.shape[0] // NX
     half = a_ref.shape[3]
@@ -223,7 +223,7 @@
     score[0] = jnp.sum(value * raw, axis=1, keepdims=True)
 
 
-def raw_blocks(scalars, rows, gate, pre, a_whole, b_group, carried):
+def raw_blocks(scalars, rows, gate, pre, a_whole, b_group):
     slots, width = rows.shape
     hid = pre.shape[1]
     block, step = hid // NZ, slots // RAW_STEPS
@@ -238,27 +238,19 @@
         pl.BlockSpec((step, block), lambda p, i, sc: (i, sc[p])),
         pl.BlockSpec((1, *a_whole.shape[1:]), lambda p, i, sc: (sc[p], 0, 0, 0)),
     ]
-    in_specs += [pl.BlockSpec(b.shape, lambda p, i, sc: (0, 0, 0)) for b in b_list]
-    args = [rows, gate, pre, a_whole, *b_list]
-    aliases = {}
-    in_specs += [pl.BlockSpec(memory_space=pl.ANY)] * 2
-    if carried is not None:
-        aliases = {1 + len(args): 0, 2 + len(args): 1}
-        args += list(carried)
-    else:
-        args += [gate, gate]
-    n = len(parts)
+    once = pl.Buffered(1)
+    in_specs += [pl.BlockSpec(b.shape, lambda p, i, sc: (0, 0, 0), pipeline_mode=once) for b in b_list]
     return pl.pallas_call(
         functools.partial(raw_kernel, parts),
         name="raw",
         out_shape=(
             jax.ShapeDtypeStruct((slots, hid), BF),
             jax.ShapeDtypeStruct((NZ * NX * extra, width), BF),
-            jax.ShapeDtypeStruct((n, slots, 1), F32),
+            jax.ShapeDtypeStruct((NZ, slots, 1), F32),
         ),
         grid_spec=pltpu.PrefetchScalarGridSpec(
             num_scalar_prefetch=1,
-            grid=(n, RAW_STEPS),
+            grid=(NZ, RAW_STEPS),
             in_specs=in_specs,
             out_specs=(
                 pl.BlockSpec((step, block), lambda p, i, sc: (i, sc[p])),
@@ -267,14 +259,11 @@
             ),
             scratch_shapes=[pltpu.VMEM((block, width), BF), pltpu.VMEM((NX * extra, width), F32)],
         ),
-        input_output_aliases=aliases,
-        compiler_params=pltpu.CompilerParams(vmem_limit_bytes=16 << 20),
+        compiler_params=pltpu.CompilerParams(vmem_limit_bytes=24 << 20),
         cost_estimate=pl.CostEstimate(
-            flops=2 * n * slots * block * width,
-            bytes_accessed=5_000_000 * n,
-            transcendentals=n * slots * block,
-        ),
-    )(scalars, *args)
+            flops=2 * slots * hid * width, bytes_accessed=22_000_000, transcendentals=slots * hid
+        ),
+    )(scalars, rows, gate, pre, a_whole, *b_list)
 
 
 def to_all(a, axis, n):
@@ -291,9 +280,9 @@
     cap = slots // n_exp
 
     shard = jnp.concatenate([routed_down[0], shared_down], axis=0)
-    a_whole = lax.all_gather(shard[:, :OFFLOADED], DP)
+    a_whole = lax.all_gather(shard[:, :GATHER_OFFLOADED], DP)
     a_whole = a_whole.reshape(NZ, NX, *a_whole.shape[1:])
-    b_shard = shard[:, OFFLOADED:]
+    b_shard = shard[:, GATHER_OFFLOADED:]
     around = [b_shard] + [hop(b_shard, "x", -k) for k in range(1, NX)]
     b_all = lax.dynamic_slice_in_dim(jnp.stack(around + around[:-1]), (NX - x) % NX, NX, 0)
     b_pieces = gather_eight(b_all, "z", cut_rows)
@@ -315,27 +304,26 @@
     ).astype(BF)
     ta, tb = terms(hidden_b, scaled, shared_term.reshape(NZ, NX, -1, width))
 
-    def along(t, place, n):
-        return lambda r: lax.dynamic_index_in_dim(t, (place + r) % n, 0, keepdims=False)
-
-    sum_a = sum_ring(along(ta, x, NX), NX, "x", cut_rows, join_rows).astype(BF)
-    sum_b = sum_ring(along(tb, z, NZ), NZ, "z", cut_rows, join_rows).astype(BF)
-    sum_a = lax.all_to_all(sum_a, "z", 0, 0, tiled=True)
+    sum_a = lax.psum_scatter(
+        ta.reshape(-1, ta.shape[3]), "x", scatter_dimension=0, tiled=True
+    )
+    sum_a = lax.psum_scatter(sum_a, "z", scatter_dimension=0, tiled=True)
+
+    def along(r):
+        return lax.dynamic_index_in_dim(tb, (z + r) % NZ, 0, keepdims=False)
+
+    sum_b = sum_ring(along, NZ, "z").astype(BF)
     sum_b = lax.all_to_all(sum_b, "x", 0, 0, tiled=True)
-    sum_a = sum_a.astype(F32).sum(axis=0)
+    sum_a = sum_a.astype(F32)
     sum_b = sum_b.astype(F32).sum(axis=0)
     total = jnp.concatenate([sum_a, sum_b], axis=1)
     rows = routed_down.shape[1]
 
-    carried, scores = None, []
-    for group in GROUPS:
-        sc = jnp.stack([(z + (NZ - j)) % NZ for j in group]).astype(jnp.int32)
-        pieces = [b_pieces[j] for j in group]
-        out, wsh, score = raw_blocks(sc, recv_rows, gate_col, pre, a_whole, pieces, carried)
-        carried = (out, wsh)
-        scores.append(score)
-    routed_pre_grad, whole_shared = carried
-    slot_score = jnp.concatenate(scores, axis=0).sum(axis=0)
+    sc = jnp.stack([(z + (NZ - j)) % NZ for j in range(NZ)]).astype(jnp.int32)
+    routed_pre_grad, whole_shared, score = raw_blocks(
+        sc, recv_rows, gate_col, pre, a_whole, b_pieces
+    )
+    slot_score = score.sum(axis=0)
     returned = lax.all_to_all(slot_score.reshape(n_exp, cap), EXPERT, 0, 0, tiled=True)
 
     labels = jnp.arange(n_exp, dtype=jnp.int32)

time: 359 us -> 364 us (1.014)
  waiting for transfers between devices: 131 us -> 184 us
  local copies, waits for them, and re-layouts: 42.1 us -> 18.9 us
  other arithmetic: 45.4 us -> 30.5 us
  starting transfers between devices: 48.5 us -> 37.4 us
    reduce_scatter x0 -> x2, waiting for transfers between devices: none -> 49.2 us  [the longest x1 49.2 us: body(): lax.psum_scatter(ta.reshape(-1, ta.shape[3]), 'x', scatter_dimension=0, t...]
    unnamed x61 -> x31, local copies, waits for them, and re-layouts: 31.1 us -> 11.9 us
    ppermute x24 -> x20, starting transfers between devices: 34.4 us -> 28.4 us  [hop(): return lax.ppermute(a, axis, [(i, (i + by) % n) for i in range(n)])]
    concatenate x4 -> x0, other arithmetic: 5.44 us -> none  [join_rows(): return jnp.concatenate([a, b], axis=0)]
    ppermute x24 -> x20, waiting for transfers between devices: 129 us -> 134 us  [hop(): return lax.ppermute(a, axis, [(i, (i + by) % n) for i in range(n)])]
    all_to_all x1 -> x0, starting transfers between devices: 4.53 us -> none  [body(): sum_a = lax.all_to_all(sum_a, 'z', 0, 0, tiled=True)]
    slice x4 -> x2, local copies, waits for them, and re-layouts: 7.68 us -> 3.41 us  [cut_rows(): return (a[:half], a[half:])]
    reduce_sum x6 -> x1, other arithmetic: 5.77 us -> 1.59 us  [body(): slot_score = score.sum(axis=0)]
  transfers between devices with their start and end apart: 28 -> 25, of which waited for: 11 -> 12; matrix products, arithmetic and copies ran while one was open for 20% -> 10% of each run, Pallas kernels for 10% -> 0%
where the time goes in v2:
time: 364 us; the launch traced here: 360 us
  waiting for transfers between devices  184 us (51%)
  Pallas kernels  37.7 us (10%)
  starting transfers between devices  37.4 us (10%)
  other arithmetic  30.5 us (8%)
  blocking collectives  25.3 us (7%)
  local copies, waits for them, and re-layouts  18.9 us (5%)
  between operations  15.7 us (4%)
  matrix products  11.2 us (3%)
    ppermute x20, waiting for transfers between devices, hop(): return lax.ppermute(a, axis, [(i, (i + by) % n) for i in range(n)])  134 us
    reduce_scatter x1, waiting for transfers between devices, body(): lax.psum_scatter(ta.reshape(-1, ta.shape[3]), 'x', scatter_dimension=0, t...  49.2 us
    ppermute x20, starting transfers between devices, hop(): return lax.ppermute(a, axis, [(i, (i + by) % n) for i in range(n)])  28.4 us
    all_to_all x1, blocking collectives, to_all(): return lax.all_to_all(many, axis, 0, 0, tiled=True)  25.3 us
    pallas_call x1, Pallas kernels, raw_blocks(): pl.pallas_call(functools.partial(raw_kernel, parts), name='raw', out_shap...  20.5 us
    pallas_call x1, Pallas kernels, terms(): pl.pallas_call(terms_kernel, name='terms', grid=(width // part, NZ), out_...  13.3 us
    unnamed x31, local copies, waits for them, and re-layouts  11.9 us
    convert_element_type x3, other arithmetic, added(): return (a.astype(F32) + b.astype(F32)).astype(BF)  10.7 us
  transfers between devices with their start and end apart: 25, of which 12 were waited for; matrix products, arithmetic and copies ran while one was open for 10% of the time, Pallas kernels for 0%

profile of v2, /device:TPU:8, one launch (start us, length us, event | category | flops | bytes accessed | tf_op | source)
XLA Modules:
  0.0 360.3 jit_solution(2722963109671234772)
XLA Ops:
  12.2 25.3 %all_to_all.19.mine = bf16[4,136,1536]{2,1,0:T(8,128)(2,1)} all-to-all(bf16[4,136,1536]{2,1,0:T(8,128)(2,1)S(1)} %broadcast_in_dim.39), channel_id=1, replica_groups=mesh['z'=8,'x'=4,'y'=4,'c'=2] {'y'}, dimensions={0} | all-to-all | bytes 3342336 | tf_op jit(solution)/shard_map/all_to_all | solution.py:271
  39.1 2.2 collective-permute-done.partner
  41.3 3.9 %dispatch.1 = (bf16[1024,1536]{1,0:T(8,128)(2,1)S(1)}, bf16[384,1536]{1,0:T(8,128)(2,1)S(1)}, bf16[384,1536]{1,0:T(8,128)(2,1)S(1)}, f32[384,1]{1,0:T(8,128)S(1)}) custom-call(s32[2]{0:T(128)S(1)} %pad_add_fusion.sc, bf16[4,136,1536]{2,1,0:T(8,128)(2,1)} %all_to_all.19.mine, bf16[4,136,1536]{2,1,0:T(8,128)(2,1)} %collective-permute-done.partner), custom_call_target="tpu_custom_call" | custom-call | flops 200000000 | bytes 10000000 | tf_op jit(solution)/shard_map/dispatch/pallas_call | solution.py:117
  45.3 3.0 convolution_convert_fusion
  48.3 13.3 %terms.1 = (bf16[4,8,120,512]{3,2,1,0:T(8,128)(2,1)S(1)}, bf16[8,4,120,1024]{3,2,1,0:T(8,128)(2,1)S(1)}) custom-call(bf16[384,3072]{1,0:T(8,128)(2,1)S(1)} %fusion.1.hidden, bf16[384,1536]{1,0:T(8,128)(2,1)S(1)} %get-tuple-element.25.scal, bf16[8,4,24,1536]{3,2,1,0:T(8,128)(2,1)S(1)} %bitcast.66), custom_call_target="tpu_custom_call" | custom-call | flops 3623878656 | bytes 20000000 | tf_op jit(solution)/shard_map/terms/pallas_call | solution.py:159
  61.6 3.1 copy-done.1
  64.7 1.9 copy-done.3
  66.7 49.2 %reduce-scatter.3.cloned.1.call-done = bf16[960,512]{1,0:T(8,128)(2,1)} async-done(((bf16[3840,512]{1,0:T(8,128)(2,1)}), bf16[960,512]{1,0:T(8,128)(2,1)}) %reduce-scatter.3.cloned.1.call-update) | async-done | bytes 983056 | tf_op jit(solution)/shard_map/reduce_scatter | solution.py:307
  116.7 2.1 dynamic-slice_bitcast_fusion
  122.1 12.1 %collective-permute-done.12 = bf16[2,120,1024]{2,1,0:T(8,128)(2,1)} collective-permute-done((bf16[2,120,1024]{2,1,0:T(8,128)(2,1)}, bf16[2,120,1024]{2,1,0:T(8,128)(2,1)}, u32[]{:S(2)}, u32[]{:S(2)}) %collective-permute-start.12) | collective-permute-done | bytes 491552 | tf_op jit(solution)/shard_map/ppermute | solution.py:26
  135.9 3.6 fusion.20
  139.7 3.7 %collective-permute-start.15 = (bf16[4,120,1024]{2,1,0:T(8,128)(2,1)}, bf16[4,120,1024]{2,1,0:T(8,128)(2,1)}, u32[]{:S(2)}, u32[]{:S(2)}) collective-permute-start(bf16[4,120,1024]{2,1,0:T(8,128)(2,1)} %get-tuple-element.45), channel_id=1, source_target_pairs={{0,224},{32,0},{64,32},{96,64},{128,96},{160,128},{192,160},{224,1... | collective-permute-start | bytes 2949128 | tf_op jit(solution)/shard_map/ppermute | solution.py:26
  146.1 28.3 %collective-permute-done.14 = bf16[4,120,1024]{2,1,0:T(8,128)(2,1)} collective-permute-done((bf16[4,120,1024]{2,1,0:T(8,128)(2,1)}, bf16[4,120,1024]{2,1,0:T(8,128)(2,1)}, u32[]{:S(2)}, u32[]{:S(2)}) %collective-permute-start.14) | collective-permute-done | bytes 983072 | tf_op jit(solution)/shard_map/ppermute | solution.py:26
  174.4 3.4 fusion.19
  177.8 1.9 collective-permute-start.16
  181.5 42.6 %collective-permute-done.16 = bf16[4,120,1024]{2,1,0:T(8,128)(2,1)S(1)} collective-permute-done((bf16[4,120,1024]{2,1,0:T(8,128)(2,1)S(1)}, bf16[4,120,1024]{2,1,0:T(8,128)(2,1)S(1)}, u32[]{:S(2)}, u32[]{:S(2)}) %collective-permute-start.16) | collective-permute-done | bytes 983072 | tf_op jit(solution)/shard_map/ppermute | solution.py:26
  224.3 3.7 %fusion.18 = (bf16[4,120,1024]{2,1,0:T(8,128)(2,1)}, bf16[4,120,1024]{2,1,0:T(8,128)(2,1)}) fusion(bf16[4,120,1024]{2,1,0:T(8,128)(2,1)S(1)} %collective-permute-done.17, bf16[8,4,120,1024]{3,2,1,0:T(8,128)(2,1)} %copy-done.1, s32[]{:T(128)S(6)} %select_n.111, bf16[4,120,1024]{2,1,0:T(8,128)(2,1)S(1)} %collective-permute-done.16, s32[]{:T(128)S(6)} %select_n.105), kind=kLoop, calls=%fused_computation.30 | loop fusion | flops 3932160 | bytes 5898248 | tf_op jit(solution)/shard_map/convert_element_type | solution.py:40
  233.4 31.6 %collective-permute-done.8.refs_8_ = bf16[4,120,640]{2,1,0:T(8,128)(2,1)} collective-permute-done((bf16[4,120,640]{2,1,0:T(8,128)(2,1)S(1)}, bf16[4,120,640]{2,1,0:T(8,128)(2,1)}, u32[]{:S(2)}, u32[]{:S(2)}) %collective-permute-start.8) | collective-permute-done | bytes 614432 | tf_op jit(solution)/shard_map/ppermute | solution.py:26
  265.0 3.0 collective-permute-start.9
  268.0 3.3 fusion.25
  271.3 4.3 %all-to-all-start.1 = ((bf16[4,120,1024]{2,1,0:T(8,128)(2,1)}), bf16[4,120,1024]{2,1,0:T(8,128)(2,1)}, u32[]{:S(2)}, u32[]{:S(2)}) async-start(bf16[4,120,1024]{2,1,0:T(8,128)(2,1)} %fusion.25), calls=%async_computation.3 | async-start | bytes 1966080 | tf_op jit(solution)/shard_map/all_to_all | solution.py:316
  275.6 3.5 collective-permute-done.9.refs_7_
  279.1 3.7 %collective-permute-start.10 = (bf16[4,120,640]{2,1,0:T(8,128)(2,1)}, bf16[4,120,640]{2,1,0:T(8,128)(2,1)}, u32[]{:S(2)}, u32[]{:S(2)}) collective-permute-start(bf16[4,120,640]{2,1,0:T(8,128)(2,1)} %collective-permute-done.9.refs_7_), channel_id=1, source_target_pairs={{0,224},{32,0},{64,32},{96,64},{128,96},{160,128},{192,160},{224,1... | collective-permute-start | bytes 1843208 | tf_op jit(solution)/shard_map/ppermute | solution.py:26
  283.1 10.0 %collective-permute-done.10.refs_6_ = bf16[4,120,640]{2,1,0:T(8,128)(2,1)} collective-permute-done((bf16[4,120,640]{2,1,0:T(8,128)(2,1)}, bf16[4,120,640]{2,1,0:T(8,128)(2,1)}, u32[]{:S(2)}, u32[]{:S(2)}) %collective-permute-start.10) | collective-permute-done | bytes 614432 | tf_op jit(solution)/shard_map/ppermute | solution.py:26
  294.8 3.7 %collective-permute-start.11 = (bf16[2,120,640]{2,1,0:T(8,128)(2,1)}, bf16[2,120,640]{2,1,0:T(8,128)(2,1)S(1)}, u32[]{:S(2)}, u32[]{:S(2)}) collective-permute-start(bf16[2,120,640]{2,1,0:T(8,128)(2,1)} %slice.43), channel_id=1, source_target_pairs={{0,224},{32,0},{64,32},{96,64},{128,96},{160,128},{192,160},{224,1... | collective-permute-start | bytes 921608 | tf_op jit(solution)/shard_map/ppermute | solution.py:26
  300.2 2.2 convert_reduce_fusion
  304.9 1.8 fusion.32
  306.7 1.8 collective-permute-done.7.refs_4_
  308.6 3.0 copy-done.2
  312.8 20.5 %raw.1 = (bf16[384,3072]{1,0:T(8,128)(2,1)}, bf16[768,1536]{1,0:T(8,128)(2,1)S(1)}, f32[8,384,1]{2,1,0:T(8,128)S(1)}) custom-call(s32[8]{0:T(128)S(1)} %stack.62.sc, bf16[384,1536]{1,0:T(8,128)(2,1)S(1)} %copy-done.6, f32[384,1]{1,0:T(8,128)S(1)} %get-tuple-element.23.gate, bf16[384,3072]{1,0:T(8,128)(2,1)S(1)} %bitcast.63, ...), custom_call_target="tpu_custom_call" | custom-call | flops 3623878656 | bytes 22000000 | tf_op jit(solution)/shard_map/raw/pallas_call | solution.py:243
  338.1 4.7 %all-to-all-start.2 = ((f32[8,1,48]{2,1,0:T(1,128)}), f32[8,1,48]{2,1,0:T(1,128)S(1)}, u32[]{:S(2)}, u32[]{:S(2)}) async-start(f32[8,1,48]{2,1,0:T(1,128)} %all_to_all.14), calls=%async_computation.4 | async-start | bytes 8192 | tf_op jit(solution)/shard_map/all_to_all | solution.py:327
  342.8 8.1 %fusion.13 = bf16[1024,768]{1,0:T(8,128)(2,1)} fusion(bf16[1024,768]{1,0:T(8,128)(2,1)} %param.12, bf16[1024,1536]{1,0:T(8,128)(2,1)} %copy-done.7, bf16[768,1536]{1,0:T(8,128)(2,1)} %copy-done.8), kind=kOutput, calls=%fused_computation.24 | convolution fusion | flops 2431647744 | bytes 8650752 | tf_op jit(solution)/shard_map/dot_general | solution.py:342
  (90 shorter events, 36.3 us)
Async XLA Ops:
  8.0 107.9 %reduce-scatter.3.cloned.1.call-start = ((), (), s32[]{:S(2)}) async-start(), calls=%async_computation.5 | async-start | bytes 4915200 | tf_op jit(solution)/shard_map/reduce_scatter | solution.py:307
  12.1 25.5 %copy-start = (bf16[1,1,384,3072]{3,2,1,0:T(8,128)(2,1)S(1)}, bf16[1,1,384,3072]{3,2,1,0:T(8,128)(2,1)}, u32[]{:S(2)}) copy-start(bf16[1,1,384,3072]{3,2,1,0:T(8,128)(2,1)} %param.10) | copy-start | bytes 7077892
  37.4 3.9 %collective-permute-start = (bf16[4,136,1536]{2,1,0:T(8,128)(2,1)}, bf16[4,136,1536]{2,1,0:T(8,128)(2,1)}, u32[]{:S(2)}, u32[]{:S(2)}) collective-permute-start(bf16[4,136,1536]{2,1,0:T(8,128)(2,1)} %all_to_all.19.mine), channel_id=1, source_target_pairs={{0,1},{1,0},{2,3},{3,2},{4,5},{5,4},{6,7},{7,6},{8,9},{9,8},{10,11... | collective-permute-start | bytes 5013512 | tf_op jit(solution)/shard_map/ppermute | solution.py:26
  39.1 6.1 %copy-start.12 = (bf16[1024,768]{1,0:T(8,128)(2,1)S(1)}, bf16[1024,768]{1,0:T(8,128)(2,1)}, u32[]{:S(2)}) copy-start(bf16[1024,768]{1,0:T(8,128)(2,1)} %param.12) | copy-start | bytes 4718596
  45.3 3.0 copy-start.5
  61.6 3.1 copy-start.1
  66.6 49.4 %copy-start.9 = (bf16[1,96,1536]{2,1,0:T(8,128)(2,1)S(1)}, bf16[1,96,1536]{2,1,0:T(8,128)(2,1)}, u32[]{:S(2)}) copy-start(bf16[1,96,1536]{2,1,0:T(8,128)(2,1)} %param.11) | copy-start | bytes 884740
  66.6 49.4 %copy-start.11 = (bf16[24,1536]{1,0:T(8,128)(2,1)S(1)}, bf16[24,1536]{1,0:T(8,128)(2,1)}, u32[]{:S(2)}) copy-start(bf16[24,1536]{1,0:T(8,128)(2,1)} %param.13) | copy-start | bytes 221188
  66.6 235.8 %reduce-scatter.5.cloned.1.call-start = ((), (), s32[]{:S(2)}) async-start(), calls=%async_computation.6 | async-start | bytes 1105920 | tf_op jit(solution)/shard_map/reduce_scatter | solution.py:310
  115.9 192.7 %all-gather.3.cloned.1.call-start = ((), (), s32[]{:S(2)}) async-start(), calls=%async_computation.7 | async-start | bytes 7096320 | tf_op jit(solution)/shard_map/all_gather | solution.py:283
  118.8 15.4 %collective-permute-start.12 = (bf16[2,120,1024]{2,1,0:T(8,128)(2,1)}, bf16[2,120,1024]{2,1,0:T(8,128)(2,1)}, u32[]{:S(2)}, u32[]{:S(2)}) collective-permute-start(bf16[2,120,1024]{2,1,0:T(8,128)(2,1)} %get-tuple-element.48), channel_id=1, source_target_pairs={{0,32},{32,64},{64,96},{96,128},{128,160},{160,192},{192,224},{224... | collective-permute-start | bytes 1474568 | tf_op jit(solution)/shard_map/ppermute | solution.py:26
  120.3 15.6 %collective-permute-start.13 = (bf16[2,120,1024]{2,1,0:T(8,128)(2,1)S(1)}, bf16[2,120,1024]{2,1,0:T(8,128)(2,1)}, u32[]{:S(2)}, u32[]{:S(2)}) collective-permute-start(bf16[2,120,1024]{2,1,0:T(8,128)(2,1)S(1)} %get-tuple-element.47), channel_id=1, source_target_pairs={{0,224},{32,0},{64,32},{96,64},{128,96},{160,128},{192,160},{224,1... | collective-permute-start | bytes 1474568 | tf_op jit(solution)/shard_map/ppermute | solution.py:26
  139.5 34.9 %collective-permute-start.14 = (bf16[4,120,1024]{2,1,0:T(8,128)(2,1)}, bf16[4,120,1024]{2,1,0:T(8,128)(2,1)}, u32[]{:S(2)}, u32[]{:S(2)}) collective-permute-start(bf16[4,120,1024]{2,1,0:T(8,128)(2,1)} %get-tuple-element.46), channel_id=1, source_target_pairs={{0,32},{32,64},{64,96},{96,128},{128,160},{160,192},{192,224},{224... | collective-permute-start | bytes 2949128 | tf_op jit(solution)/shard_map/ppermute | solution.py:26
  139.7 34.7 %collective-permute-start.15 = (bf16[4,120,1024]{2,1,0:T(8,128)(2,1)}, bf16[4,120,1024]{2,1,0:T(8,128)(2,1)}, u32[]{:S(2)}, u32[]{:S(2)}) collective-permute-start(bf16[4,120,1024]{2,1,0:T(8,128)(2,1)} %get-tuple-element.45), channel_id=1, source_target_pairs={{0,224},{32,0},{64,32},{96,64},{128,96},{160,128},{192,160},{224,1... | collective-permute-start | bytes 2949128 | tf_op jit(solution)/shard_map/ppermute | solution.py:26
  144.0 37.3 %collective-permute-start.1 = (bf16[120,640]{1,0:T(8,128)(2,1)S(1)}, bf16[120,640]{1,0:T(8,128)(2,1)S(1)}, u32[]{:S(2)}, u32[]{:S(2)}) collective-permute-start(bf16[120,640]{1,0:T(8,128)(2,1)S(1)} %get-tuple-element.40), channel_id=1, source_target_pairs={{0,24},{8,0},{16,8},{24,16},{1,25},{9,1},{17,9},{25,17},{2,26},{10... | collective-permute-start | bytes 460808 | tf_op jit(solution)/shard_map/ppermute | solution.py:26
  144.1 37.3 %collective-permute-start.2 = (bf16[120,640]{1,0:T(8,128)(2,1)S(1)}, bf16[120,640]{1,0:T(8,128)(2,1)S(1)}, u32[]{:S(2)}, u32[]{:S(2)}) collective-permute-start(bf16[120,640]{1,0:T(8,128)(2,1)S(1)} %get-tuple-element.40), channel_id=1, source_target_pairs={{0,16},{8,24},{16,0},{24,8},{1,17},{9,25},{17,1},{25,9},{2,18},{10... | collective-permute-start | bytes 460808 | tf_op jit(solution)/shard_map/ppermute | solution.py:26
  145.1 36.2 %collective-permute-start.3 = (bf16[120,640]{1,0:T(8,128)(2,1)S(1)}, bf16[120,640]{1,0:T(8,128)(2,1)S(1)}, u32[]{:S(2)}, u32[]{:S(2)}) collective-permute-start(bf16[120,640]{1,0:T(8,128)(2,1)S(1)} %get-tuple-element.40), channel_id=1, source_target_pairs={{0,8},{8,16},{16,24},{24,0},{1,9},{9,17},{17,25},{25,1},{2,10},{10... | collective-permute-start | bytes 460808 | tf_op jit(solution)/shard_map/ppermute | solution.py:26
  146.1 35.2 %copy-start.10 = (bf16[7,120,640]{2,1,0:T(8,128)(2,1)S(1)}, bf16[7,120,640]{2,1,0:T(8,128)(2,1)}, u32[]{:S(2)}) copy-start(bf16[7,120,640]{2,1,0:T(8,128)(2,1)} %get-tuple-element.39) | copy-start | bytes 3225604
  177.8 46.3 %collective-permute-start.16 = (bf16[4,120,1024]{2,1,0:T(8,128)(2,1)S(1)}, bf16[4,120,1024]{2,1,0:T(8,128)(2,1)S(1)}, u32[]{:S(2)}, u32[]{:S(2)}) collective-permute-start(bf16[4,120,1024]{2,1,0:T(8,128)(2,1)S(1)} %get-tuple-element.44), channel_id=1, source_target_pairs={{0,32},{32,64},{64,96},{96,128},{128,160},{160,192},{192,224},{224... | collective-permute-start | bytes 2949128 | tf_op jit(solution)/shard_map/ppermute | solution.py:26
  179.7 44.6 %collective-permute-start.17 = (bf16[4,120,1024]{2,1,0:T(8,128)(2,1)S(1)}, bf16[4,120,1024]{2,1,0:T(8,128)(2,1)S(1)}, u32[]{:S(2)}, u32[]{:S(2)}) collective-permute-start(bf16[4,120,1024]{2,1,0:T(8,128)(2,1)S(1)} %get-tuple-element.43), channel_id=1, source_target_pairs={{0,224},{32,0},{64,32},{96,64},{128,96},{160,128},{192,160},{224,1... | collective-permute-start | bytes 2949128 | tf_op jit(solution)/shard_map/ppermute | solution.py:26
  228.0 40.0 %collective-permute-start.18 = (bf16[4,120,1024]{2,1,0:T(8,128)(2,1)}, bf16[4,120,1024]{2,1,0:T(8,128)(2,1)}, u32[]{:S(2)}, u32[]{:S(2)}) collective-permute-start(bf16[4,120,1024]{2,1,0:T(8,128)(2,1)} %get-tuple-element.42), channel_id=1, source_target_pairs={{0,32},{32,64},{64,96},{96,128},{128,160},{160,192},{192,224},{224... | collective-permute-start | bytes 2949128 | tf_op jit(solution)/shard_map/ppermute | solution.py:26
  229.6 38.4 %collective-permute-start.19 = (bf16[4,120,1024]{2,1,0:T(8,128)(2,1)}, bf16[4,120,1024]{2,1,0:T(8,128)(2,1)}, u32[]{:S(2)}, u32[]{:S(2)}) collective-permute-start(bf16[4,120,1024]{2,1,0:T(8,128)(2,1)} %get-tuple-element.41), channel_id=1, source_target_pairs={{0,224},{32,0},{64,32},{96,64},{128,96},{160,128},{192,160},{224,1... | collective-permute-start | bytes 2949128 | tf_op jit(solution)/shard_map/ppermute | solution.py:26
  231.3 33.7 %collective-permute-start.8 = (bf16[4,120,640]{2,1,0:T(8,128)(2,1)S(1)}, bf16[4,120,640]{2,1,0:T(8,128)(2,1)}, u32[]{:S(2)}, u32[]{:S(2)}) collective-permute-start(bf16[4,120,640]{2,1,0:T(8,128)(2,1)S(1)} %constant_dynamic-slice_fusion.refs_0_), channel_id=1, source_target_pairs={{0,224},{32,0},{64,32},{96,64},{128,96},{160,128},{192,160},{224,1... | collective-permute-start | bytes 1843208 | tf_op jit(solution)/shard_map/ppermute | solution.py:26
  231.6 36.3 %collective-permute-start.4 = (bf16[4,120,640]{2,1,0:T(8,128)(2,1)S(1)}, bf16[4,120,640]{2,1,0:T(8,128)(2,1)}, u32[]{:S(2)}, u32[]{:S(2)}) collective-permute-start(bf16[4,120,640]{2,1,0:T(8,128)(2,1)S(1)} %constant_dynamic-slice_fusion.refs_0_), channel_id=1, source_target_pairs={{0,32},{32,64},{64,96},{96,128},{128,160},{160,192},{192,224},{224... | collective-permute-start | bytes 1843208 | tf_op jit(solution)/shard_map/ppermute | solution.py:26
  265.0 14.1 %collective-permute-start.9 = (bf16[4,120,640]{2,1,0:T(8,128)(2,1)}, bf16[4,120,640]{2,1,0:T(8,128)(2,1)}, u32[]{:S(2)}, u32[]{:S(2)}) collective-permute-start(bf16[4,120,640]{2,1,0:T(8,128)(2,1)} %collective-permute-done.8.refs_8_), channel_id=1, source_target_pairs={{0,224},{32,0},{64,32},{96,64},{128,96},{160,128},{192,160},{224,1... | collective-permute-start | bytes 1843208 | tf_op jit(solution)/shard_map/ppermute | solution.py:26
  268.0 15.0 %collective-permute-start.5 = (bf16[4,120,640]{2,1,0:T(8,128)(2,1)}, bf16[4,120,640]{2,1,0:T(8,128)(2,1)}, u32[]{:S(2)}, u32[]{:S(2)}) collective-permute-start(bf16[4,120,640]{2,1,0:T(8,128)(2,1)} %collective-permute-done.4.refs_1_), channel_id=1, source_target_pairs={{0,32},{32,64},{64,96},{96,128},{128,160},{160,192},{192,224},{224... | collective-permute-start | bytes 1843208 | tf_op jit(solution)/shard_map/ppermute | solution.py:26
  271.3 28.9 %all-to-all-start.1 = ((bf16[4,120,1024]{2,1,0:T(8,128)(2,1)}), bf16[4,120,1024]{2,1,0:T(8,128)(2,1)}, u32[]{:S(2)}, u32[]{:S(2)}) async-start(bf16[4,120,1024]{2,1,0:T(8,128)(2,1)} %fusion.25), calls=%async_computation.3 | async-start | bytes 1966080 | tf_op jit(solution)/shard_map/all_to_all | solution.py:316
  279.1 14.0 %collective-permute-start.10 = (bf16[4,120,640]{2,1,0:T(8,128)(2,1)}, bf16[4,120,640]{2,1,0:T(8,128)(2,1)}, u32[]{:S(2)}, u32[]{:S(2)}) collective-permute-start(bf16[4,120,640]{2,1,0:T(8,128)(2,1)} %collective-permute-done.9.refs_7_), channel_id=1, source_target_pairs={{0,224},{32,0},{64,32},{96,64},{128,96},{160,128},{192,160},{224,1... | collective-permute-start | bytes 1843208 | tf_op jit(solution)/shard_map/ppermute | solution.py:26
  283.0 15.5 %collective-permute-start.6 = (bf16[4,120,640]{2,1,0:T(8,128)(2,1)}, bf16[4,120,640]{2,1,0:T(8,128)(2,1)}, u32[]{:S(2)}, u32[]{:S(2)}) collective-permute-start(bf16[4,120,640]{2,1,0:T(8,128)(2,1)} %collective-permute-done.5.refs_2_), channel_id=1, source_target_pairs={{0,32},{32,64},{64,96},{96,128},{128,160},{160,192},{192,224},{224... | collective-permute-start | bytes 1843208 | tf_op jit(solution)/shard_map/ppermute | solution.py:26
  294.8 11.9 %collective-permute-start.11 = (bf16[2,120,640]{2,1,0:T(8,128)(2,1)}, bf16[2,120,640]{2,1,0:T(8,128)(2,1)S(1)}, u32[]{:S(2)}, u32[]{:S(2)}) collective-permute-start(bf16[2,120,640]{2,1,0:T(8,128)(2,1)} %slice.43), channel_id=1, source_target_pairs={{0,224},{32,0},{64,32},{96,64},{128,96},{160,128},{192,160},{224,1... | collective-permute-start | bytes 921608 | tf_op jit(solution)/shard_map/ppermute | solution.py:26
  300.2 8.4 %collective-permute-start.7 = (bf16[2,120,640]{2,1,0:T(8,128)(2,1)}, bf16[2,120,640]{2,1,0:T(8,128)(2,1)}, u32[]{:S(2)}, u32[]{:S(2)}) collective-permute-start(bf16[2,120,640]{2,1,0:T(8,128)(2,1)} %slice.42), channel_id=1, source_target_pairs={{0,32},{32,64},{64,96},{96,128},{128,160},{160,192},{192,224},{224... | collective-permute-start | bytes 921608 | tf_op jit(solution)/shard_map/ppermute | solution.py:26
  338.1 12.8 %all-to-all-start.2 = ((f32[8,1,48]{2,1,0:T(1,128)}), f32[8,1,48]{2,1,0:T(1,128)S(1)}, u32[]{:S(2)}, u32[]{:S(2)}) async-start(f32[8,1,48]{2,1,0:T(1,128)} %all_to_all.14), calls=%async_computation.4 | async-start | bytes 8192 | tf_op jit(solution)/shard_map/all_to_all | solution.py:327
  (6 other events, 11.7 us)
Sparse Core Ops, SparseCore 0:
  66.8 49.0 reduce-scatter.2
  118.4 46.4 reduce-scatter.4
Sparse Core Ops, SparseCore 1:
  119.0 116.2 all-gather.2

commit v3 on v2

--- a/solution.py
+++ b/solution.py
@@ -1,5 +1,3 @@
-import functools
-
 import jax
 import jax.numpy as jnp
 from jax import lax
@@ -40,32 +38,34 @@
     return (a.astype(F32) + b.astype(F32)).astype(BF)
 
 
-def gather_eight(a, axis, cut):
-    right = [a]
-    left = [a]
-    for _ in range(1, 4):
+def ring_gather(a, axis, dim):
+    n = lax.axis_size(axis)
+    half = a.shape[dim] // 2
+    right, left = [a], [a]
+    for _ in range(1, n // 2):
         right.append(hop(right[-1], axis, 1))
         left.append(hop(left[-1], axis, -1))
-    far = (hop(cut(right[3])[0], axis, 1), hop(cut(left[3])[1], axis, -1))
-    return right[0], right[1], right[2], right[3], far, left[3], left[2], left[1]
-
-
-def cut_rows(a):
-    half = a.shape[0] // 2
-    return a[:half], a[half:]
-
-
-def sum_ring(block, n, axis):
+    first = lax.slice_in_dim(right[-1], 0, half, axis=dim)
+    second = lax.slice_in_dim(left[-1], half, 2 * half, axis=dim)
+    far = (hop(first, axis, 1), hop(second, axis, -1))
+    return right, far, left[:0:-1]
+
+
+def sum_ring(block, n, axis, dim):
     far = block(n // 2)
-    half = far.shape[0] // 2
-    right = hop(far[:half], axis, 1)
-    left = hop(far[half:], axis, -1)
-    rest = ((0, 0),) * (far.ndim - 1)
+    half = far.shape[dim] // 2
+    first = lax.slice_in_dim(far, 0, half, axis=dim)
+    second = lax.slice_in_dim(far, half, 2 * half, axis=dim)
+    right = hop(first, axis, 1)
+    left = hop(second, axis, -1)
     for k, r in enumerate(range(n // 2 - 1, 0, -1)):
         right, left = lax.optimization_barrier((right, left))
         if k == 0:
-            right = jnp.pad(right, ((0, half), *rest))
-            left = jnp.pad(left, ((half, 0), *rest))
+            grown = [(0, 0)] * far.ndim
+            grown[dim] = (0, half)
+            right = jnp.pad(right, grown)
+            grown[dim] = (half, 0)
+            left = jnp.pad(left, grown)
         right = hop(added(block(r), right), axis, 1)
         left = hop(added(block(n - r), left), axis, -1)
     right, left = lax.optimization_barrier((right, left))
@@ -135,48 +135,36 @@
     out = lax.dot_general(
         hidden[...], scal[...], (((0,), (0,)), ((), ())), preferred_element_type=F32
     )
-    nx, part = tb.shape[1], tb.shape[3]
+    nx, half = ta.shape[1], ta.shape[3]
     rows = hidden.shape[1] // nx
-    out = out.astype(BF).reshape(nx, rows, part)
-
-    @pl.when(pl.program_id(0) == 0)
-    def _():
-        ta[:, 0, :rows, :] = out
-        ta[:, 0, rows:, :] = tsh[0]
-
-    @pl.when(pl.program_id(0) > 0)
-    def _():
-        tb[0, :, :rows, :] = out
-        tb[0, :, rows:, :] = tsh[0]
+    out = out.astype(BF).reshape(nx, rows, 2 * half)
+    ta[0, :, :rows, :] = out[:, :, :half]
+    tb[:, 0, :rows, :] = out[:, :, half:]
+    ta[0, :, rows:, :] = tsh[0, :, :, :half]
+    tb[:, 0, rows:, :] = tsh[0, :, :, half:]
 
 
 def terms(hidden, scal, tsh):
     slots, hid = hidden.shape
     width = scal.shape[1]
-    part = SUMS_OFFLOADED
     rows, extra = hid // (NZ * NX), tsh.shape[2]
-    high = rows + extra
+    tail = (rows + extra, width // 2)
     return pl.pallas_call(
         terms_kernel,
         name="terms",
-        grid=(width // part, NZ),
+        grid=(NZ,),
         out_shape=(
-            jax.ShapeDtypeStruct((NX, NZ, high, part), BF),
-            jax.ShapeDtypeStruct((NZ, NX, high, width - part), BF),
+            jax.ShapeDtypeStruct((NZ, NX, *tail), BF),
+            jax.ShapeDtypeStruct((NX, NZ, *tail), BF),
         ),
         in_specs=[
-            pl.BlockSpec((slots, hid // NZ), lambda j, k: (0, k)),
-            pl.BlockSpec((slots, part), lambda j, k: (0, j)),
-            pl.BlockSpec((1, NX, extra, part), lambda j, k: (k, 0, 0, j)),
+            pl.BlockSpec((slots, hid // NZ), lambda k: (0, k)),
+            pl.BlockSpec((slots, width), lambda k: (0, 0)),
+            pl.BlockSpec((1, NX, extra, width), lambda k: (k, 0, 0, 0)),
         ],
         out_specs=(
-            pl.BlockSpec(
-                (NX, 1, high, part), lambda j, k: (0, jnp.where(j == 0, k, NZ - 1), 0, 0)
-            ),
-            pl.BlockSpec(
-                (1, NX, high, part),
-                lambda j, k: (jnp.where(j == 0, 0, k), 0, 0, jnp.maximum(j - 1, 0)),
-            ),
+            pl.BlockSpec((1, NX, *tail), lambda k: (k, 0, 0, 0)),
+            pl.BlockSpec((NX, 1, *tail), lambda k: (0, k, 0, 0)),
         ),
         compiler_params=pltpu.CompilerParams(vmem_limit_bytes=24 << 20),
         cost_estimate=pl.CostEstimate(
@@ -186,32 +174,37 @@
 
 
 RAW_STEPS = 3
-GATHER_OFFLOADED = 896
-SUMS_OFFLOADED = 512
-
-
-def raw_kernel(parts, sc, rows, gate, pre, a_ref, *refs):
-    *b_refs, out, wsh, score, whole, small = refs
+
+
+def raw_kernel(sc, rows, gate, pre, a_ref, own, right, far0, far1, left, out, wsh, score, whole, small):
     n_rows = whole.shape[0] // NX
     extra = small.shape[0] // NX
     half = a_ref.shape[3]
+    x = sc[NZ]
+
+    def put(ref, r):
+        source = (x + (NX - r)) % NX
+        at = pl.ds(pl.multiple_of(source * n_rows, n_rows), n_rows)
+        whole[at, half:] = ref[0, :n_rows, :]
+        at = pl.ds(pl.multiple_of(source * extra, extra), extra)
+        small[at, half:] = ref[0, n_rows:, :].astype(F32)
 
     @pl.when(pl.program_id(1) == 0)
     def _():
         for k in range(NX):
             whole[k * n_rows : (k + 1) * n_rows, :half] = a_ref[0, k, :n_rows, :]
             small[k * extra : (k + 1) * extra, :half] = a_ref[0, k, n_rows:, :].astype(F32)
-        at = 0
-        for p, n in enumerate(parts):
-            mine = b_refs[at : at + n]
-            at += n
-
-            @pl.when(pl.program_id(0) == p)
-            def _():
-                for k in range(NX):
-                    b_ref, i = mine[k * n // NX], k % (NX // n)
-                    whole[k * n_rows : (k + 1) * n_rows, half:] = b_ref[i, :n_rows, :]
-                    small[k * extra : (k + 1) * extra, half:] = b_ref[i, n_rows:, :].astype(F32)
+        put(own, 0)
+        put(right, 1)
+        put(left, 3)
+
+        @pl.when(pl.program_id(0) < NZ // 2)
+        def _():
+            put(far0, 2)
+
+        @pl.when(pl.program_id(0) >= NZ // 2)
+        def _():
+            put(far1, 2)
 
         wsh[...] = small[...].astype(BF)
 
@@ -223,25 +216,16 @@
     score[0] = jnp.sum(value * raw, axis=1, keepdims=True)
 
 
-def raw_blocks(scalars, rows, gate, pre, a_whole, b_group):
+def raw_blocks(scalars, rows, gate, pre, a_whole, own, right, far, left):
     slots, width = rows.shape
     hid = pre.shape[1]
     block, step = hid // NZ, slots // RAW_STEPS
     n_rows = block // NX
     extra = a_whole.shape[2] - n_rows
-    b_group = [list(b) if isinstance(b, tuple) else [b] for b in b_group]
-    parts = tuple(len(b) for b in b_group)
-    b_list = sum(b_group, [])
-    in_specs = [
-        pl.BlockSpec((step, width), lambda p, i, sc: (i, 0)),
-        pl.BlockSpec((step, 1), lambda p, i, sc: (i, 0)),
-        pl.BlockSpec((step, block), lambda p, i, sc: (i, sc[p])),
-        pl.BlockSpec((1, *a_whole.shape[1:]), lambda p, i, sc: (sc[p], 0, 0, 0)),
-    ]
-    once = pl.Buffered(1)
-    in_specs += [pl.BlockSpec(b.shape, lambda p, i, sc: (0, 0, 0), pipeline_mode=once) for b in b_list]
+    piece = (1, *own.shape[1:])
+    here = pl.BlockSpec(piece, lambda p, i, sc: (p, 0, 0))
     return pl.pallas_call(
-        functools.partial(raw_kernel, parts),
+        raw_kernel,
         name="raw",
         out_shape=(
             jax.ShapeDtypeStruct((slots, hid), BF),
@@ -251,7 +235,17 @@
         grid_spec=pltpu.PrefetchScalarGridSpec(
             num_scalar_prefetch=1,
             grid=(NZ, RAW_STEPS),
-            in_specs=in_specs,
+            in_specs=[
+                pl.BlockSpec((step, width), lambda p, i, sc: (i, 0)),
+                pl.BlockSpec((step, 1), lambda p, i, sc: (i, 0)),
+                pl.BlockSpec((step, block), lambda p, i, sc: (i, sc[p])),
+                pl.BlockSpec((1, *a_whole.shape[1:]), lambda p, i, sc: (sc[p], 0, 0, 0)),
+                here,
+                here,
+                pl.BlockSpec(piece, lambda p, i, sc: (jnp.minimum(p, NZ // 2 - 1), 0, 0)),
+                pl.BlockSpec(piece, lambda p, i, sc: (jnp.maximum(p - NZ // 2, 0), 0, 0)),
+                here,
+            ],
             out_specs=(
                 pl.BlockSpec((step, block), lambda p, i, sc: (i, sc[p])),
                 pl.BlockSpec((NX * extra, width), lambda p, i, sc: (sc[p], 0)),
@@ -263,7 +257,7 @@
         cost_estimate=pl.CostEstimate(
             flops=2 * slots * hid * width, bytes_accessed=22_000_000, transcendentals=slots * hid
         ),
-    )(scalars, rows, gate, pre, a_whole, *b_list)
+    )(scalars, rows, gate, pre, a_whole, own, right, *far, left)
 
 
 def to_all(a, axis, n):
@@ -280,12 +274,12 @@
     cap = slots // n_exp
 
     shard = jnp.concatenate([routed_down[0], shared_down], axis=0)
-    a_whole = lax.all_gather(shard[:, :GATHER_OFFLOADED], DP)
+    half = width // 2
+    a_whole = lax.all_gather(shard[:, :half], DP)
     a_whole = a_whole.reshape(NZ, NX, *a_whole.shape[1:])
-    b_shard = shard[:, GATHER_OFFLOADED:]
-    around = [b_shard] + [hop(b_shard, "x", -k) for k in range(1, NX)]
-    b_all = lax.dynamic_slice_in_dim(jnp.stack(around + around[:-1]), (NX - x) % NX, NX, 0)
-    b_pieces = gather_eight(b_all, "z", cut_rows)
+    right, far, left = ring_gather(shard[:, half:], "z", 1)
+    b_column = jnp.stack([*right, jnp.concatenate(far, axis=1), *left], axis=0)
+    b_pieces = ring_gather(b_column, "x", 0)
 
     metas = jnp.concatenate([gates.astype(BF).T, expert_ids.astype(BF).T], axis=0)
     metas = jnp.pad(metas, ((0, 8 - metas.shape[0]), (0, width - tok)))
@@ -304,36 +298,35 @@
     ).astype(BF)
     ta, tb = terms(hidden_b, scaled, shared_term.reshape(NZ, NX, -1, width))
 
-    sum_a = lax.psum_scatter(
-        ta.reshape(-1, ta.shape[3]), "x", scatter_dimension=0, tiled=True
-    )
-    sum_a = lax.psum_scatter(sum_a, "z", scatter_dimension=0, tiled=True)
-
-    def along(r):
-        return lax.dynamic_index_in_dim(tb, (z + r) % NZ, 0, keepdims=False)
-
-    sum_b = sum_ring(along, NZ, "z").astype(BF)
-    sum_b = lax.all_to_all(sum_b, "x", 0, 0, tiled=True)
+    sum_a = lax.psum_scatter(ta.reshape(-1, half), "z", scatter_dimension=0, tiled=True)
+    sum_a = lax.psum_scatter(sum_a, "x", scatter_dimension=0, tiled=True)
     sum_a = sum_a.astype(F32)
-    sum_b = sum_b.astype(F32).sum(axis=0)
+
+    def along(t, place, n):
+        return lambda r: lax.dynamic_index_in_dim(t, (place + r) % n, 0, keepdims=False)
+
+    sum_b = sum_ring(along(tb, x, NX), NX, "x", 0).astype(BF)
+    sum_b = sum_ring(along(sum_b, z, NZ), NZ, "z", 1)
     total = jnp.concatenate([sum_a, sum_b], axis=1)
     rows = routed_down.shape[1]
 
-    sc = jnp.stack([(z + (NZ - j)) % NZ for j in range(NZ)]).astype(jnp.int32)
+    sc = jnp.stack([(z + (NZ - j)) % NZ for j in range(NZ)] + [x]).astype(jnp.int32)
+    (own, right), far, (left,) = b_pieces
     routed_pre_grad, whole_shared, score = raw_blocks(
-        sc, recv_rows, gate_col, pre, a_whole, b_pieces
+        sc, recv_rows, gate_col, pre, a_whole, own, right, far, left
     )
     slot_score = score.sum(axis=0)
     returned = lax.all_to_all(slot_score.reshape(n_exp, cap), EXPERT, 0, 0, tiled=True)
 
+    own_ids = lax.optimization_barrier((expert_ids, gate_col))[0]
     labels = jnp.arange(n_exp, dtype=jnp.int32)
-    onehot = expert_ids[:, :, None] == labels[None, None, :]
+    onehot = own_ids[:, :, None] == labels[None, None, :]
     named = jnp.any(onehot, axis=1).astype(F32)
     order = jnp.arange(tok, dtype=jnp.int32)
     tri = (order[None, :] < order[:, None]).astype(F32)
     counts = lax.dot_general(tri, named, (((1,), (0,)), ((), ())), preferred_element_type=F32)
     rank = jnp.sum(jnp.where(onehot, counts[:, None, :], 0.0), axis=2).astype(jnp.int32)
-    slot = expert_ids * cap + rank
+    slot = own_ids * cap + rank
     each = jnp.arange(slots, dtype=jnp.int32)
     gate_grad = jnp.sum(
         jnp.where(slot[:, :, None] == each[None, None, :], returned.reshape(1, 1, slots), 0.0), axis=2

time: 364 us -> 286 us (0.79)
  waiting for transfers between devices: 184 us -> 96.2 us
  starting transfers between devices: 37.4 us -> 48.6 us
  local copies, waits for them, and re-layouts: 18.9 us -> 27.9 us
  other arithmetic: 30.5 us -> 24.8 us
    reduce_scatter x2, waiting for transfers between devices: 49.2 us -> 0.01 us  [the longest x1 0.01 us: body(): lax.psum_scatter(ta.reshape(-1, half), 'z', scatter_dimension=0, tiled=True)]
    ppermute x20 -> x25, waiting for transfers between devices: 134 us -> 96.1 us  [hop(): return lax.ppermute(a, axis, [(i, (i + by) % n) for i in range(n)])]
    ppermute x20 -> x25, starting transfers between devices: 28.4 us -> 44.3 us  [hop(): return lax.ppermute(a, axis, [(i, (i + by) % n) for i in range(n)])]
    unnamed x31 -> x39, local copies, waits for them, and re-layouts: 11.9 us -> 17.4 us
    all_to_all x1 -> x0, starting transfers between devices: 4.26 us -> none  [body(): sum_b = lax.all_to_all(sum_b, 'x', 0, 0, tiled=True)]
    convert_element_type x3 -> x4, other arithmetic: 10.7 us -> 7.32 us  [added(): return (a.astype(F32) + b.astype(F32)).astype(BF)]
    slice x3 -> x6, local copies, waits for them, and re-layouts: 5.46 us -> 7.4 us  [the longest x2 3.3 us: sum_ring(): second = lax.slice_in_dim(far, half, 2 * half, axis=dim)]
  transfers between devices with their start and end apart: 25 -> 29, of which waited for: 12 -> 14; matrix products, arithmetic and copies ran while one was open for 10% -> 15% of each run, Pallas kernels for 0% -> 8%
where the time goes in v3:
time: 286 us; the launch traced here: 284 us
  waiting for transfers between devices  96.2 us (34%)
  starting transfers between devices  48.6 us (17%)
  Pallas kernels  34.2 us (12%)
  local copies, waits for them, and re-layouts  27.9 us (10%)
  blocking collectives  25.1 us (9%)
  other arithmetic  24.8 us (9%)
  between operations  15.8 us (6%)
  matrix products  11.3 us (4%)
    ppermute x25, waiting for transfers between devices, hop(): return lax.ppermute(a, axis, [(i, (i + by) % n) for i in range(n)])  96.1 us
    ppermute x25, starting transfers between devices, hop(): return lax.ppermute(a, axis, [(i, (i + by) % n) for i in range(n)])  44.3 us
    all_to_all x1, blocking collectives, to_all(): return lax.all_to_all(many, axis, 0, 0, tiled=True)  25.1 us
    pallas_call x1, Pallas kernels, raw_blocks(): pl.pallas_call(raw_kernel, name='raw', out_shape=(jax.ShapeDtypeStruct((s...  23.3 us
    unnamed x39, local copies, waits for them, and re-layouts  17.4 us
    dot_general x1, matrix products, body(): lax.dot_general(group_rows, whole_shared, (((1,), (1,)), ((), ())), prefe...  8.15 us
    convert_element_type x4, other arithmetic, added(): return (a.astype(F32) + b.astype(F32)).astype(BF)  7.32 us
    pallas_call x1, Pallas kernels, terms(): pl.pallas_call(terms_kernel, name='terms', grid=(NZ,), out_shape=(jax.Sha...  6.99 us
  transfers between devices with their start and end apart: 29, of which 14 were waited for; matrix products, arithmetic and copies ran while one was open for 15% of the time, Pallas kernels for 8%

profile of v3, /device:TPU:8, one launch (start us, length us, event | category | flops | bytes accessed | tf_op | source)
XLA Modules:
  0.0 283.9 jit_solution(7687748713617892743)
XLA Ops:
  10.7 25.1 %all_to_all.14.mine = bf16[4,136,1536]{2,1,0:T(8,128)(2,1)} all-to-all(bf16[4,136,1536]{2,1,0:T(8,128)(2,1)S(1)} %broadcast_in_dim.39), channel_id=1, replica_groups=mesh['z'=8,'x'=4,'y'=4,'c'=2] {'y'}, dimensions={0} | all-to-all | bytes 3342336 | tf_op jit(solution)/shard_map/all_to_all | solution.py:265
  39.7 3.9 %dispatch.1 = (bf16[1024,1536]{1,0:T(8,128)(2,1)S(1)}, bf16[384,1536]{1,0:T(8,128)(2,1)S(1)}, bf16[384,1536]{1,0:T(8,128)(2,1)S(1)}, f32[384,1]{1,0:T(8,128)S(1)}) custom-call(s32[2]{0:T(128)S(1)} %pad_add_fusion.sc, bf16[4,136,1536]{2,1,0:T(8,128)(2,1)} %all_to_all.14.mine, bf16[4,136,1536]{2,1,0:T(8,128)(2,1)} %collective-permute-done.partner), custom_call_target="tpu_custom_call" | custom-call | flops 200000000 | bytes 10000000 | tf_op jit(solution)/shard_map/dispatch/pallas_call | solution.py:117
  43.7 3.0 %convolution_convert_fusion = bf16[768,1536]{1,0:T(8,128)(2,1)S(1)} fusion(bf16[1024,1536]{1,0:T(8,128)(2,1)S(1)} %get-tuple-element.31, bf16[1024,768]{1,0:T(8,128)(2,1)S(1)} %copy-done.16), kind=kOutput, calls=%fused_computation.18 | convolution fusion | flops 2424963072 | bytes 7077888 | tf_op jit(solution)/shard_map/dot_general | solution.py:296
  46.7 7.0 %terms.1 = (bf16[8,4,120,768]{3,2,1,0:T(8,128)(2,1)S(1)}, bf16[4,8,120,768]{3,2,1,0:T(8,128)(2,1)S(1)}) custom-call(bf16[384,3072]{1,0:T(8,128)(2,1)S(1)} %fusion.1.hidden, bf16[384,1536]{1,0:T(8,128)(2,1)S(1)} %get-tuple-element.30.scal, bf16[8,4,24,1536]{3,2,1,0:T(8,128)(2,1)S(1)} %bitcast.85), custom_call_target="tpu_custom_call" | custom-call | flops 3623878656 | bytes 20000000 | tf_op jit(solution)/shard_map/terms/pallas_call | solution.py:152
  53.7 2.5 copy-done.2
  56.2 2.5 copy-done.3
  60.6 2.6 dynamic-slice_bitcast_fusion
  69.1 3.9 %collective-permute-start.5 = (bf16[120,768]{1,0:T(8,128)(2,1)}, bf16[120,768]{1,0:T(8,128)(2,1)}, u32[]{:S(2)}, u32[]{:S(2)}) collective-permute-start(bf16[120,768]{1,0:T(8,128)(2,1)} %get-tuple-element.50), channel_id=1, source_target_pairs={{0,224},{32,0},{64,32},{96,64},{128,96},{160,128},{192,160},{224,1... | collective-permute-start | bytes 552968 | tf_op jit(solution)/shard_map/ppermute | solution.py:24
  73.0 7.7 %collective-permute-done.1 = bf16[120,768]{1,0:T(8,128)(2,1)} collective-permute-done((bf16[120,768]{1,0:T(8,128)(2,1)}, bf16[120,768]{1,0:T(8,128)(2,1)}, u32[]{:S(2)}, u32[]{:S(2)}) %collective-permute-start.1) | collective-permute-done | bytes 184352 | tf_op jit(solution)/shard_map/ppermute | solution.py:24
  81.8 3.7 %collective-permute-start.6 = (bf16[120,768]{1,0:T(8,128)(2,1)}, bf16[120,768]{1,0:T(8,128)(2,1)S(1)}, u32[]{:S(2)}, u32[]{:S(2)}) collective-permute-start(bf16[120,768]{1,0:T(8,128)(2,1)} %collective-permute-done.5), channel_id=1, source_target_pairs={{0,224},{32,0},{64,32},{96,64},{128,96},{160,128},{192,160},{224,1... | collective-permute-start | bytes 552968 | tf_op jit(solution)/shard_map/ppermute | solution.py:24
  87.1 5.2 %collective-permute-done.2 = bf16[120,768]{1,0:T(8,128)(2,1)S(1)} collective-permute-done((bf16[120,768]{1,0:T(8,128)(2,1)}, bf16[120,768]{1,0:T(8,128)(2,1)S(1)}, u32[]{:S(2)}, u32[]{:S(2)}) %collective-permute-start.2) | collective-permute-done | bytes 184352 | tf_op jit(solution)/shard_map/ppermute | solution.py:24
  94.1 3.6 %collective-permute-start.7 = (bf16[120,768]{1,0:T(8,128)(2,1)S(1)}, bf16[120,768]{1,0:T(8,128)(2,1)S(1)}, u32[]{:S(2)}, u32[]{:S(2)}) collective-permute-start(bf16[120,768]{1,0:T(8,128)(2,1)S(1)} %collective-permute-done.6), channel_id=1, source_target_pairs={{0,224},{32,0},{64,32},{96,64},{128,96},{160,128},{192,160},{224,1... | collective-permute-start | bytes 552968 | tf_op jit(solution)/shard_map/ppermute | solution.py:24
  98.3 5.2 %collective-permute-done.3 = bf16[120,768]{1,0:T(8,128)(2,1)S(1)} collective-permute-done((bf16[120,768]{1,0:T(8,128)(2,1)S(1)}, bf16[120,768]{1,0:T(8,128)(2,1)S(1)}, u32[]{:S(2)}, u32[]{:S(2)}) %collective-permute-start.3) | collective-permute-done | bytes 184352 | tf_op jit(solution)/shard_map/ppermute | solution.py:24
  105.7 3.8 %collective-permute-start.8 = (bf16[120,384]{1,0:T(8,128)(2,1)S(1)}, bf16[120,384]{1,0:T(8,128)(2,1)S(1)}, u32[]{:S(2)}, u32[]{:S(2)}) collective-permute-start(bf16[120,384]{1,0:T(8,128)(2,1)S(1)} %slice.59), channel_id=1, source_target_pairs={{0,224},{32,0},{64,32},{96,64},{128,96},{160,128},{192,160},{224,1... | collective-permute-start | bytes 276488 | tf_op jit(solution)/shard_map/ppermute | solution.py:24
  109.5 4.2 %fusion.18 = (bf16[8,120,768]{2,1,0:T(8,128)(2,1)}, bf16[8,120,768]{2,1,0:T(8,128)(2,1)}) fusion(bf16[4,120,768]{2,1,0:T(8,128)(2,1)} %collective-permute-done.14, bf16[4,8,120,768]{3,2,1,0:T(8,128)(2,1)} %copy-done.3, s32[]{:T(128)S(6)} %select_n.130, bf16[4,120,768]{2,1,0:T(8,128)(2,1)} %collective-permute-done.13, s32[]{:T(128)S(6)} %select_n.126), kind=kLoop, calls=%fused_computation.30 | loop fusion | flops 5898240 | bytes 7372808 | tf_op jit(solution)/shard_map/convert_element_type | solution.py:38
  113.7 3.2 %collective-permute-start.16 = (bf16[8,120,768]{2,1,0:T(8,128)(2,1)}, bf16[8,120,768]{2,1,0:T(8,128)(2,1)}, u32[]{:S(2)}, u32[]{:S(2)}) collective-permute-start(bf16[8,120,768]{2,1,0:T(8,128)(2,1)} %get-tuple-element.51), channel_id=1, source_target_pairs={{0,24},{8,0},{16,8},{24,16},{1,25},{9,1},{17,9},{25,17},{2,26},{10... | collective-permute-start | bytes 4423688 | tf_op jit(solution)/shard_map/ppermute | solution.py:24
  121.3 3.2 %collective-permute-start.11 = (bf16[8,120,768]{2,1,0:T(8,128)(2,1)}, bf16[8,120,768]{2,1,0:T(8,128)(2,1)}, u32[]{:S(2)}, u32[]{:S(2)}) collective-permute-start(bf16[8,120,768]{2,1,0:T(8,128)(2,1)} %bitcast_dynamic-update-slice_fusion.own), channel_id=1, source_target_pairs={{0,24},{8,0},{16,8},{24,16},{1,25},{9,1},{17,9},{25,17},{2,26},{10... | collective-permute-start | bytes 4423688 | tf_op jit(solution)/shard_map/ppermute | solution.py:24
  124.5 25.8 %collective-permute-done.15 = bf16[8,120,768]{2,1,0:T(8,128)(2,1)} collective-permute-done((bf16[8,120,768]{2,1,0:T(8,128)(2,1)}, bf16[8,120,768]{2,1,0:T(8,128)(2,1)}, u32[]{:S(2)}, u32[]{:S(2)}) %collective-permute-start.15) | collective-permute-done | bytes 1474592 | tf_op jit(solution)/shard_map/ppermute | solution.py:24
  150.3 2.8 fusion.21
  154.9 3.2 %collective-permute-start.18 = (bf16[120,384]{1,0:T(8,128)(2,1)}, bf16[120,384]{1,0:T(8,128)(2,1)}, u32[]{:S(2)}, u32[]{:S(2)}) collective-permute-start(bf16[120,384]{1,0:T(8,128)(2,1)} %get-tuple-element.61), channel_id=1, source_target_pairs={{0,224},{32,0},{64,32},{96,64},{128,96},{160,128},{192,160},{224,1... | collective-permute-start | bytes 276488 | tf_op jit(solution)/shard_map/ppermute | solution.py:24
  158.2 3.7 %collective-permute-done.17 = bf16[120,384]{1,0:T(8,128)(2,1)} collective-permute-done((bf16[120,384]{1,0:T(8,128)(2,1)}, bf16[120,384]{1,0:T(8,128)(2,1)}, u32[]{:S(2)}, u32[]{:S(2)}) %collective-permute-start.17) | collective-permute-done | bytes 92192 | tf_op jit(solution)/shard_map/ppermute | solution.py:24
  164.8 3.7 %collective-permute-start.20 = (bf16[120,768]{1,0:T(8,128)(2,1)}, bf16[120,768]{1,0:T(8,128)(2,1)}, u32[]{:S(2)}, u32[]{:S(2)}) collective-permute-start(bf16[120,768]{1,0:T(8,128)(2,1)} %get-tuple-element.59), channel_id=1, source_target_pairs={{0,224},{32,0},{64,32},{96,64},{128,96},{160,128},{192,160},{224,1... | collective-permute-start | bytes 552968 | tf_op jit(solution)/shard_map/ppermute | solution.py:24
  168.6 29.8 %collective-permute-done.9.right = bf16[8,120,768]{2,1,0:T(8,128)(2,1)} collective-permute-done((bf16[8,120,768]{2,1,0:T(8,128)(2,1)}, bf16[8,120,768]{2,1,0:T(8,128)(2,1)}, u32[]{:S(2)}, u32[]{:S(2)}) %collective-permute-start.9) | collective-permute-done | bytes 1474592 | tf_op jit(solution)/shard_map/ppermute | solution.py:24
  202.7 3.7 %collective-permute-start.12 = (bf16[4,120,768]{2,1,0:T(8,128)(2,1)}, bf16[4,120,768]{2,1,0:T(8,128)(2,1)}, u32[]{:S(2)}, u32[]{:S(2)}) collective-permute-start(bf16[4,120,768]{2,1,0:T(8,128)(2,1)} %slice.61), channel_id=1, source_target_pairs={{0,24},{8,0},{16,8},{24,16},{1,25},{9,1},{17,9},{25,17},{2,26},{10... | collective-permute-start | bytes 2211848 | tf_op jit(solution)/shard_map/ppermute | solution.py:24
  207.6 3.2 %collective-permute-start.22 = (bf16[120,768]{1,0:T(8,128)(2,1)S(1)}, bf16[120,768]{1,0:T(8,128)(2,1)S(1)}, u32[]{:S(2)}, u32[]{:S(2)}) collective-permute-start(bf16[120,768]{1,0:T(8,128)(2,1)S(1)} %get-tuple-element.57), channel_id=1, source_target_pairs={{0,224},{32,0},{64,32},{96,64},{128,96},{160,128},{192,160},{224,1... | collective-permute-start | bytes 552968 | tf_op jit(solution)/shard_map/ppermute | solution.py:24
  211.0 7.0 %collective-permute-done.21 = bf16[120,768]{1,0:T(8,128)(2,1)S(1)} collective-permute-done((bf16[120,768]{1,0:T(8,128)(2,1)S(1)}, bf16[120,768]{1,0:T(8,128)(2,1)S(1)}, u32[]{:S(2)}, u32[]{:S(2)}) %collective-permute-start.21) | collective-permute-done | bytes 184352 | tf_op jit(solution)/shard_map/ppermute | solution.py:24
  218.5 3.2 %collective-permute-start.24 = (bf16[120,768]{1,0:T(8,128)(2,1)S(1)}, bf16[120,768]{1,0:T(8,128)(2,1)}, u32[]{:S(2)}, u32[]{:S(2)}) collective-permute-start(bf16[120,768]{1,0:T(8,128)(2,1)S(1)} %get-tuple-element.55), channel_id=1, source_target_pairs={{0,224},{32,0},{64,32},{96,64},{128,96},{160,128},{192,160},{224,1... | collective-permute-start | bytes 552968 | tf_op jit(solution)/shard_map/ppermute | solution.py:24
  221.7 3.5 %collective-permute-done.23 = bf16[120,768]{1,0:T(8,128)(2,1)S(1)} collective-permute-done((bf16[120,768]{1,0:T(8,128)(2,1)S(1)}, bf16[120,768]{1,0:T(8,128)(2,1)S(1)}, u32[]{:S(2)}, u32[]{:S(2)}) %collective-permute-start.23) | collective-permute-done | bytes 184352 | tf_op jit(solution)/shard_map/ppermute | solution.py:24
  227.9 2.7 copy-done.1
  231.5 23.3 %raw.1 = (bf16[384,3072]{1,0:T(8,128)(2,1)}, bf16[768,1536]{1,0:T(8,128)(2,1)S(1)}, f32[8,384,1]{2,1,0:T(8,128)S(1)}) custom-call(s32[9]{0:T(128)S(1)} %stack.75.sc, bf16[384,1536]{1,0:T(8,128)(2,1)S(1)} %get-tuple-element.27.rows, f32[384,1]{1,0:T(8,128)S(1)} %copy-done.6, bf16[384,3072]{1,0:T(8,128)(2,1)S(1)} %bitcast.82, ...), custom_call_target="tpu_custom_call" | custom-call | flops 3623878656 | bytes 22000000 | tf_op jit(solution)/shard_map/raw/pallas_call | solution.py:227
  259.6 4.1 %all-to-all-start.1 = ((f32[8,1,48]{2,1,0:T(1,128)}), f32[8,1,48]{2,1,0:T(1,128)S(1)}, u32[]{:S(2)}, u32[]{:S(2)}) async-start(f32[8,1,48]{2,1,0:T(1,128)} %all_to_all.10), calls=%async_computation.3 | async-start | bytes 8192 | tf_op jit(solution)/shard_map/all_to_all | solution.py:319
  263.8 8.1 %fusion.13 = bf16[1024,768]{1,0:T(8,128)(2,1)} fusion(bf16[1024,768]{1,0:T(8,128)(2,1)} %param.12, bf16[1024,1536]{1,0:T(8,128)(2,1)} %copy-done.7, bf16[768,1536]{1,0:T(8,128)(2,1)} %copy-done.8), kind=kOutput, calls=%fused_computation.24 | convolution fusion | flops 2431647744 | bytes 8650752 | tf_op jit(solution)/shard_map/dot_general | solution.py:335
  (112 shorter events, 49.8 us)
Async XLA Ops:
  8.0 217.9 %reduce-scatter.3.cloned.1.call-start = ((), (), s32[]{:S(2)}) async-start(), calls=%async_computation.4 | async-start | bytes 6635520 | tf_op jit(solution)/shard_map/reduce_scatter | solution.py:301
  9.4 26.5 %copy-start = (bf16[1,1,384,3072]{3,2,1,0:T(8,128)(2,1)S(1)}, bf16[1,1,384,3072]{3,2,1,0:T(8,128)(2,1)}, u32[]{:S(2)}) copy-start(bf16[1,1,384,3072]{3,2,1,0:T(8,128)(2,1)} %param.10) | copy-start | bytes 7077892
  35.9 3.9 %collective-permute-start = (bf16[4,136,1536]{2,1,0:T(8,128)(2,1)}, bf16[4,136,1536]{2,1,0:T(8,128)(2,1)}, u32[]{:S(2)}, u32[]{:S(2)}) collective-permute-start(bf16[4,136,1536]{2,1,0:T(8,128)(2,1)} %all_to_all.14.mine), channel_id=1, source_target_pairs={{0,1},{1,0},{2,3},{3,2},{4,5},{5,4},{6,7},{7,6},{8,9},{9,8},{10,11... | collective-permute-start | bytes 5013512 | tf_op jit(solution)/shard_map/ppermute | solution.py:24
  58.8 169.1 %all-gather.3.cloned.1.call-start = ((), (), s32[]{:S(2)}) async-start(), calls=%async_computation.6 | async-start | bytes 6082560 | tf_op jit(solution)/shard_map/all_gather | solution.py:278
  60.5 213.5 %reduce-scatter.5.cloned.1.call-start = ((), (), s32[]{:S(2)}) async-start(), calls=%async_computation.5 | async-start | bytes 921600 | tf_op jit(solution)/shard_map/reduce_scatter | solution.py:302
  63.2 46.3 %collective-permute-start.13 = (bf16[4,120,768]{2,1,0:T(8,128)(2,1)}, bf16[4,120,768]{2,1,0:T(8,128)(2,1)}, u32[]{:S(2)}, u32[]{:S(2)}) collective-permute-start(bf16[4,120,768]{2,1,0:T(8,128)(2,1)} %get-tuple-element.54), channel_id=1, source_target_pairs={{0,8},{8,16},{16,24},{24,0},{1,9},{9,17},{17,25},{25,1},{2,10},{10... | collective-permute-start | bytes 2211848 | tf_op jit(solution)/shard_map/ppermute | solution.py:24
  64.7 44.8 %collective-permute-start.14 = (bf16[4,120,768]{2,1,0:T(8,128)(2,1)}, bf16[4,120,768]{2,1,0:T(8,128)(2,1)}, u32[]{:S(2)}, u32[]{:S(2)}) collective-permute-start(bf16[4,120,768]{2,1,0:T(8,128)(2,1)} %get-tuple-element.53), channel_id=1, source_target_pairs={{0,24},{8,0},{16,8},{24,16},{1,25},{9,1},{17,9},{25,17},{2,26},{10... | collective-permute-start | bytes 2211848 | tf_op jit(solution)/shard_map/ppermute | solution.py:24
  67.2 13.6 %collective-permute-start.1 = (bf16[120,768]{1,0:T(8,128)(2,1)}, bf16[120,768]{1,0:T(8,128)(2,1)}, u32[]{:S(2)}, u32[]{:S(2)}) collective-permute-start(bf16[120,768]{1,0:T(8,128)(2,1)} %get-tuple-element.50), channel_id=1, source_target_pairs={{0,32},{32,64},{64,96},{96,128},{128,160},{160,192},{192,224},{224... | collective-permute-start | bytes 552968 | tf_op jit(solution)/shard_map/ppermute | solution.py:24
  69.1 12.7 %collective-permute-start.5 = (bf16[120,768]{1,0:T(8,128)(2,1)}, bf16[120,768]{1,0:T(8,128)(2,1)}, u32[]{:S(2)}, u32[]{:S(2)}) collective-permute-start(bf16[120,768]{1,0:T(8,128)(2,1)} %get-tuple-element.50), channel_id=1, source_target_pairs={{0,224},{32,0},{64,32},{96,64},{128,96},{160,128},{192,160},{224,1... | collective-permute-start | bytes 552968 | tf_op jit(solution)/shard_map/ppermute | solution.py:24
  80.7 11.5 %collective-permute-start.2 = (bf16[120,768]{1,0:T(8,128)(2,1)}, bf16[120,768]{1,0:T(8,128)(2,1)S(1)}, u32[]{:S(2)}, u32[]{:S(2)}) collective-permute-start(bf16[120,768]{1,0:T(8,128)(2,1)} %collective-permute-done.1), channel_id=1, source_target_pairs={{0,32},{32,64},{64,96},{96,128},{128,160},{160,192},{192,224},{224... | collective-permute-start | bytes 552968 | tf_op jit(solution)/shard_map/ppermute | solution.py:24
  81.8 12.2 %collective-permute-start.6 = (bf16[120,768]{1,0:T(8,128)(2,1)}, bf16[120,768]{1,0:T(8,128)(2,1)S(1)}, u32[]{:S(2)}, u32[]{:S(2)}) collective-permute-start(bf16[120,768]{1,0:T(8,128)(2,1)} %collective-permute-done.5), channel_id=1, source_target_pairs={{0,224},{32,0},{64,32},{96,64},{128,96},{160,128},{192,160},{224,1... | collective-permute-start | bytes 552968 | tf_op jit(solution)/shard_map/ppermute | solution.py:24
  92.3 11.2 %collective-permute-start.3 = (bf16[120,768]{1,0:T(8,128)(2,1)S(1)}, bf16[120,768]{1,0:T(8,128)(2,1)S(1)}, u32[]{:S(2)}, u32[]{:S(2)}) collective-permute-start(bf16[120,768]{1,0:T(8,128)(2,1)S(1)} %collective-permute-done.2), channel_id=1, source_target_pairs={{0,32},{32,64},{64,96},{96,128},{128,160},{160,192},{192,224},{224... | collective-permute-start | bytes 552968 | tf_op jit(solution)/shard_map/ppermute | solution.py:24
  94.1 11.6 %collective-permute-start.7 = (bf16[120,768]{1,0:T(8,128)(2,1)S(1)}, bf16[120,768]{1,0:T(8,128)(2,1)S(1)}, u32[]{:S(2)}, u32[]{:S(2)}) collective-permute-start(bf16[120,768]{1,0:T(8,128)(2,1)S(1)} %collective-permute-done.6), channel_id=1, source_target_pairs={{0,224},{32,0},{64,32},{96,64},{128,96},{160,128},{192,160},{224,1... | collective-permute-start | bytes 552968 | tf_op jit(solution)/shard_map/ppermute | solution.py:24
  103.5 14.1 %collective-permute-start.4 = (bf16[120,384]{1,0:T(8,128)(2,1)S(1)}, bf16[120,384]{1,0:T(8,128)(2,1)S(1)}, u32[]{:S(2)}, u32[]{:S(2)}) collective-permute-start(bf16[120,384]{1,0:T(8,128)(2,1)S(1)} %slice.58), channel_id=1, source_target_pairs={{0,32},{32,64},{64,96},{96,128},{128,160},{160,192},{192,224},{224... | collective-permute-start | bytes 276488 | tf_op jit(solution)/shard_map/ppermute | solution.py:24
  105.7 11.9 %collective-permute-start.8 = (bf16[120,384]{1,0:T(8,128)(2,1)S(1)}, bf16[120,384]{1,0:T(8,128)(2,1)S(1)}, u32[]{:S(2)}, u32[]{:S(2)}) collective-permute-start(bf16[120,384]{1,0:T(8,128)(2,1)S(1)} %slice.59), channel_id=1, source_target_pairs={{0,224},{32,0},{64,32},{96,64},{128,96},{160,128},{192,160},{224,1... | collective-permute-start | bytes 276488 | tf_op jit(solution)/shard_map/ppermute | solution.py:24
  113.7 36.6 %collective-permute-start.15 = (bf16[8,120,768]{2,1,0:T(8,128)(2,1)}, bf16[8,120,768]{2,1,0:T(8,128)(2,1)}, u32[]{:S(2)}, u32[]{:S(2)}) collective-permute-start(bf16[8,120,768]{2,1,0:T(8,128)(2,1)} %get-tuple-element.52), channel_id=1, source_target_pairs={{0,8},{8,16},{16,24},{24,0},{1,9},{9,17},{17,25},{25,1},{2,10},{10... | collective-permute-start | bytes 4423688 | tf_op jit(solution)/shard_map/ppermute | solution.py:24
  113.7 36.6 %collective-permute-start.16 = (bf16[8,120,768]{2,1,0:T(8,128)(2,1)}, bf16[8,120,768]{2,1,0:T(8,128)(2,1)}, u32[]{:S(2)}, u32[]{:S(2)}) collective-permute-start(bf16[8,120,768]{2,1,0:T(8,128)(2,1)} %get-tuple-element.51), channel_id=1, source_target_pairs={{0,24},{8,0},{16,8},{24,16},{1,25},{9,1},{17,9},{25,17},{2,26},{10... | collective-permute-start | bytes 4423688 | tf_op jit(solution)/shard_map/ppermute | solution.py:24
  121.3 77.2 %collective-permute-start.9 = (bf16[8,120,768]{2,1,0:T(8,128)(2,1)}, bf16[8,120,768]{2,1,0:T(8,128)(2,1)}, u32[]{:S(2)}, u32[]{:S(2)}) collective-permute-start(bf16[8,120,768]{2,1,0:T(8,128)(2,1)} %bitcast_dynamic-update-slice_fusion.own), channel_id=1, source_target_pairs={{0,8},{8,16},{16,24},{24,0},{1,9},{9,17},{17,25},{25,1},{2,10},{10... | collective-permute-start | bytes 4423688 | tf_op jit(solution)/shard_map/ppermute | solution.py:24
  121.3 79.4 %collective-permute-start.11 = (bf16[8,120,768]{2,1,0:T(8,128)(2,1)}, bf16[8,120,768]{2,1,0:T(8,128)(2,1)}, u32[]{:S(2)}, u32[]{:S(2)}) collective-permute-start(bf16[8,120,768]{2,1,0:T(8,128)(2,1)} %bitcast_dynamic-update-slice_fusion.own), channel_id=1, source_target_pairs={{0,24},{8,0},{16,8},{24,16},{1,25},{9,1},{17,9},{25,17},{2,26},{10... | collective-permute-start | bytes 4423688 | tf_op jit(solution)/shard_map/ppermute | solution.py:24
  154.2 52.2 %copy-start.15 = (s32[128,2]{0,1:T(2,128)S(1)}, s32[128,2]{0,1:T(2,128)}, u32[]{:S(2)}) copy-start(s32[128,2]{0,1:T(2,128)} %param.8) | copy-start | bytes 3076
  154.9 6.9 %collective-permute-start.17 = (bf16[120,384]{1,0:T(8,128)(2,1)}, bf16[120,384]{1,0:T(8,128)(2,1)}, u32[]{:S(2)}, u32[]{:S(2)}) collective-permute-start(bf16[120,384]{1,0:T(8,128)(2,1)} %get-tuple-element.62), channel_id=1, source_target_pairs={{0,32},{32,64},{64,96},{96,128},{128,160},{160,192},{192,224},{224... | collective-permute-start | bytes 276488 | tf_op jit(solution)/shard_map/ppermute | solution.py:24
  154.9 8.0 %collective-permute-start.18 = (bf16[120,384]{1,0:T(8,128)(2,1)}, bf16[120,384]{1,0:T(8,128)(2,1)}, u32[]{:S(2)}, u32[]{:S(2)}) collective-permute-start(bf16[120,384]{1,0:T(8,128)(2,1)} %get-tuple-element.61), channel_id=1, source_target_pairs={{0,224},{32,0},{64,32},{96,64},{128,96},{160,128},{192,160},{224,1... | collective-permute-start | bytes 276488 | tf_op jit(solution)/shard_map/ppermute | solution.py:24
  164.8 41.6 %collective-permute-start.19 = (bf16[120,768]{1,0:T(8,128)(2,1)}, bf16[120,768]{1,0:T(8,128)(2,1)}, u32[]{:S(2)}, u32[]{:S(2)}) collective-permute-start(bf16[120,768]{1,0:T(8,128)(2,1)} %get-tuple-element.60), channel_id=1, source_target_pairs={{0,32},{32,64},{64,96},{96,128},{128,160},{160,192},{192,224},{224... | collective-permute-start | bytes 552968 | tf_op jit(solution)/shard_map/ppermute | solution.py:24
  164.8 41.6 %collective-permute-start.20 = (bf16[120,768]{1,0:T(8,128)(2,1)}, bf16[120,768]{1,0:T(8,128)(2,1)}, u32[]{:S(2)}, u32[]{:S(2)}) collective-permute-start(bf16[120,768]{1,0:T(8,128)(2,1)} %get-tuple-element.59), channel_id=1, source_target_pairs={{0,224},{32,0},{64,32},{96,64},{128,96},{160,128},{192,160},{224,1... | collective-permute-start | bytes 552968 | tf_op jit(solution)/shard_map/ppermute | solution.py:24
  168.6 37.8 %copy-start.10 = (bf16[8,120,768]{2,1,0:T(8,128)(2,1)S(1)}, bf16[8,120,768]{2,1,0:T(8,128)(2,1)}, u32[]{:S(2)}) copy-start(bf16[8,120,768]{2,1,0:T(8,128)(2,1)} %copy-done.9) | copy-start | bytes 4423684
  200.5 27.4 %collective-permute-start.10 = (bf16[4,120,768]{2,1,0:T(8,128)(2,1)}, bf16[4,120,768]{2,1,0:T(8,128)(2,1)}, u32[]{:S(2)}, u32[]{:S(2)}) collective-permute-start(bf16[4,120,768]{2,1,0:T(8,128)(2,1)} %slice.60), channel_id=1, source_target_pairs={{0,8},{8,16},{16,24},{24,0},{1,9},{9,17},{17,25},{25,1},{2,10},{10... | collective-permute-start | bytes 2211848 | tf_op jit(solution)/shard_map/ppermute | solution.py:24
  202.7 25.1 %collective-permute-start.12 = (bf16[4,120,768]{2,1,0:T(8,128)(2,1)}, bf16[4,120,768]{2,1,0:T(8,128)(2,1)}, u32[]{:S(2)}, u32[]{:S(2)}) collective-permute-start(bf16[4,120,768]{2,1,0:T(8,128)(2,1)} %slice.61), channel_id=1, source_target_pairs={{0,24},{8,0},{16,8},{24,16},{1,25},{9,1},{17,9},{25,17},{2,26},{10... | collective-permute-start | bytes 2211848 | tf_op jit(solution)/shard_map/ppermute | solution.py:24
  207.5 10.5 %collective-permute-start.21 = (bf16[120,768]{1,0:T(8,128)(2,1)S(1)}, bf16[120,768]{1,0:T(8,128)(2,1)S(1)}, u32[]{:S(2)}, u32[]{:S(2)}) collective-permute-start(bf16[120,768]{1,0:T(8,128)(2,1)S(1)} %get-tuple-element.58), channel_id=1, source_target_pairs={{0,32},{32,64},{64,96},{96,128},{128,160},{160,192},{192,224},{224... | collective-permute-start | bytes 552968 | tf_op jit(solution)/shard_map/ppermute | solution.py:24
  207.6 10.4 %collective-permute-start.22 = (bf16[120,768]{1,0:T(8,128)(2,1)S(1)}, bf16[120,768]{1,0:T(8,128)(2,1)S(1)}, u32[]{:S(2)}, u32[]{:S(2)}) collective-permute-start(bf16[120,768]{1,0:T(8,128)(2,1)S(1)} %get-tuple-element.57), channel_id=1, source_target_pairs={{0,224},{32,0},{64,32},{96,64},{128,96},{160,128},{192,160},{224,1... | collective-permute-start | bytes 552968 | tf_op jit(solution)/shard_map/ppermute | solution.py:24
  218.2 7.0 %collective-permute-start.23 = (bf16[120,768]{1,0:T(8,128)(2,1)S(1)}, bf16[120,768]{1,0:T(8,128)(2,1)S(1)}, u32[]{:S(2)}, u32[]{:S(2)}) collective-permute-start(bf16[120,768]{1,0:T(8,128)(2,1)S(1)} %get-tuple-element.56), channel_id=1, source_target_pairs={{0,32},{32,64},{64,96},{96,128},{128,160},{160,192},{192,224},{224... | collective-permute-start | bytes 552968 | tf_op jit(solution)/shard_map/ppermute | solution.py:24
  218.5 7.4 %collective-permute-start.24 = (bf16[120,768]{1,0:T(8,128)(2,1)S(1)}, bf16[120,768]{1,0:T(8,128)(2,1)}, u32[]{:S(2)}, u32[]{:S(2)}) collective-permute-start(bf16[120,768]{1,0:T(8,128)(2,1)S(1)} %get-tuple-element.55), channel_id=1, source_target_pairs={{0,224},{32,0},{64,32},{96,64},{128,96},{160,128},{192,160},{224,1... | collective-permute-start | bytes 552968 | tf_op jit(solution)/shard_map/ppermute | solution.py:24
  259.6 12.3 %all-to-all-start.1 = ((f32[8,1,48]{2,1,0:T(1,128)}), f32[8,1,48]{2,1,0:T(1,128)S(1)}, u32[]{:S(2)}, u32[]{:S(2)}) async-start(f32[8,1,48]{2,1,0:T(1,128)} %all_to_all.10), calls=%async_computation.3 | async-start | bytes 8192 | tf_op jit(solution)/shard_map/all_to_all | solution.py:319
  (14 other events, 49.7 us)
Sparse Core Ops, SparseCore 0:
  58.9 91.6 reduce-scatter.2
  226.1 19.9 reduce-scatter.4
Sparse Core Ops, SparseCore 1:
  61.9 156.5 all-gather.2
